TPU v7x, 128 devices: a whole 4x4x4 slice. The times are simulated.
128 devices in a mesh: xline: 4 (over x), inline: 32 (over y, z, core).
Axes of the slice: x: 4, y: 4, z: 4, core: 2. Of those that a mesh axis runs over, the one named last changes fastest.
Arguments:
- pressure: float32 [1024, 256, 256], P('inline', 'xline'), may hold values from -6 to 6
- vel_inline: float32 [1024, 256, 256], P('inline', 'xline'), may hold values from -6 to 6
- vel_xline: float32 [1024, 256, 256], P('inline', 'xline'), may hold values from -6 to 6
- vel_depth: float32 [1024, 256, 256], P('inline', 'xline'), may hold values from -6 to 6
- modulus: float32 [1024, 256, 256], P('inline', 'xline'), may hold values from 0.5 to 1.5
- buoyancy: float32 [1024, 256, 256], P('inline', 'xline'), may hold values from 0.5 to 1.5
- traces: float32 [98304, 512], P(('xline', 'inline')), may hold values from -6 to 6
- owner: int32 [98304, 1], P(('xline', 'inline')), may hold values from 0 to 127; in each aligned block of 768 rows (0 to 767, 768 to 1535, ...) at most 15 rows name the same one
- node_cell: int32 [98304], P(('xline', 'inline')), may hold values from 0 to 524287
- resample: float32 [4, 512], replicated, may hold values from -0.25 to 0.25
Outputs:
- pressure_out: float32 [1024, 256, 256], P('inline', 'xline')
- inline_out: float32 [1024, 256, 256], P('inline', 'xline')
- xline_out: float32 [1024, 256, 256], P('inline', 'xline')
- depth_out: float32 [1024, 256, 256], P('inline', 'xline')
Inputs may be any that keep to these rules, and one draw needn't show every extreme that they name: Among the nodes of one device, at most 15 have the same owner.
All inputs are finite; a program needn't handle non-finite values.
Results may differ from a plain program's by a relative error of at most 0.0002.
Values sent between devices are 32-bit elements; how exact they have to be, the bound alone decides.
A program may use at most 128 MiB of HBM per device.

v0:
```python
import jax
import jax.numpy as jnp
from jax import lax
from jax.experimental import pallas as pl
from jax.experimental.pallas import tpu as pltpu
from jax.sharding import PartitionSpec as P

COURANT = 0.35
STEPS = 4
LANES = 128
SUBLANES = 8
SLOT = 8
MESH = pl.DeviceIdType.MESH
VMEM, HBM = pltpu.MemorySpace.VMEM, pltpu.MemorySpace.HBM
F32 = jnp.float32


def lane_ids():
    return lax.broadcasted_iota(jnp.int32, (SUBLANES, LANES), 1)


def row_ids():
    return lax.broadcasted_iota(jnp.int32, (SUBLANES, LANES), 0)


def cols(half):
    return pl.ds(half * LANES, LANES)


def rows(tile):
    return pl.ds(tile * SUBLANES, SUBLANES)


def velocity(p, v_in, v_out, buoyancy, i, tile, next_plane):
    lane = lane_ids()
    (vi, vx, vd), (vi_out, vx_out, vd_out) = v_in, v_out
    here = [p[i, rows(tile), cols(h)] for h in range(2)]
    turned = [pltpu.roll(x, LANES - 1, 1) for x in here]
    deeper = [jnp.where(lane < LANES - 1, turned[0], turned[1]), jnp.where(lane < LANES - 1, turned[1], 0.0)]
    last = p.shape[1] // SUBLANES - 1
    for h in range(2):
        rb = COURANT * buoyancy[i, rows(tile), cols(h)]
        vd_out[i, rows(tile), cols(h)] = vd[i, rows(tile), cols(h)] - rb * (deeper[h] - here[h])
        if next_plane:
            ahead = p[i + 1, rows(tile), cols(h)]
            vi_out[i, rows(tile), cols(h)] = vi[i, rows(tile), cols(h)] - rb * (ahead - here[h])
        if tile < last:
            ahead = p[i, pl.ds(tile * SUBLANES + 1, SUBLANES), cols(h)]
            vx_out[i, rows(tile), cols(h)] = vx[i, rows(tile), cols(h)] - rb * (ahead - here[h])


def velocity_inside(p, v_in, v_out, buoyancy):
    planes, tiles = p.shape[0], p.shape[1] // SUBLANES

    def plane(i, _):
        for tile in range(tiles):
            velocity(p, v_in, v_out, buoyancy, i, tile, True)
        return _

    lax.fori_loop(0, planes - 1, plane, 0)
    for tile in range(tiles):
        velocity(p, v_in, v_out, buoyancy, planes - 1, tile, False)


def velocity_edge(p, v_in, v_out, buoyancy, ahead_i, ahead_x):
    planes, tiles = p.shape[0], p.shape[1] // SUBLANES
    (vi, vx, _), (vi_out, vx_out, _) = v_in, v_out
    i = planes - 1
    for tile in range(tiles):
        for h in range(2):
            at = (i, rows(tile), cols(h))
            rb = COURANT * buoyancy[at]
            vi_out[at] = vi[at] - rb * (ahead_i[rows(tile), cols(h)] - p[at])
    row = row_ids()

    def plane(i, _):
        for h in range(2):
            at = (i, rows(tiles - 1), cols(h))
            here = p[at]
            ahead = jnp.where(
                row < SUBLANES - 1,
                pltpu.roll(here, SUBLANES - 1, 0),
                jnp.broadcast_to(ahead_x[h, pl.ds(i, 1), :], here.shape),
            )
            vx_out[at] = vx[at] - COURANT * buoyancy[at] * (ahead - here)
        return _

    lax.fori_loop(0, planes, plane, 0, unroll=4)


def ghosts(p, first_x, behind_i, behind_x, ghost_in, ghost_out, ghost_b):
    (vi, vx), (vi_out, vx_out), (bi, bx) = ghost_in, ghost_out, ghost_b
    vi_out[...] = vi[...] - COURANT * bi[...] * (p[0] - behind_i[...])
    vx_out[...] = vx[...] - COURANT * bx[...] * (first_x[...] - behind_x[...])


def pressure(p_in, p_out, v, ghost, modulus, i, tile, first, source):
    lane, row = lane_ids(), row_ids()
    vi, vx, vd = v
    ghost_i, ghost_x = ghost
    here = [vd[i, rows(tile), cols(h)] for h in range(2)]
    turned = [pltpu.roll(x, 1, 1) for x in here]
    upper = [jnp.where(lane > 0, turned[0], 0.0), jnp.where(lane > 0, turned[1], turned[0])]
    for h in range(2):
        at = (i, rows(tile), cols(h))
        before_i = ghost_i[rows(tile), cols(h)] if first else vi[i - 1, rows(tile), cols(h)]
        now_x = vx[at]
        if tile > 0:
            before_x = vx[i, pl.ds(tile * SUBLANES - 1, SUBLANES), cols(h)]
        else:
            before_x = jnp.where(
                row > 0,
                pltpu.roll(now_x, 1, 0),
                jnp.broadcast_to(ghost_x[h, pl.ds(i, 1), :], now_x.shape),
            )
        total = (vi[at] - before_i) + (now_x - before_x) + (here[h] - upper[h])
        if source is not None:
            total = total - source(i, tile, h)
        p_out[at] = p_in[at] - COURANT * modulus[at] * total


def shell(planes, tiles, strip):
    for tile in range(tiles):
        strip(0, tile, True)
        strip(planes - 1, tile, False)

    def plane(i, _):
        strip(i, 0, False)
        strip(i, tiles - 1, False)
        return _

    lax.fori_loop(1, planes - 1, plane, 0, unroll=2)


def core(planes, tiles, strip):
    def plane(i, _):
        for tile in range(1, tiles - 1):
            strip(i, tile, False)
        return _

    lax.fori_loop(1, planes - 1, plane, 0)


def take_row(source, row, target):
    def plane(i, _):
        for h in range(2):
            target[h, pl.ds(i, 1), :] = source[i, pl.ds(row, 1), cols(h)]
        return _

    lax.fori_loop(0, source.shape[0], plane, 0, unroll=8)


class Exchange:
    def __init__(self, send_sems, recv_sems):
        self.send_sems, self.recv_sems = send_sems, recv_sems
        self.place = (lax.axis_index("xline"), lax.axis_index("inline"))
        self.count = (lax.axis_size("xline"), lax.axis_size("inline"))
        self.copies = []

    def has(self, axis, step):
        return self.place[axis] < self.count[axis] - 1 if step > 0 else self.place[axis] > 0

    def partner(self, axis, step):
        there = list(self.place)
        there[axis] = jnp.clip(there[axis] + step, 0, self.count[axis] - 1)
        return tuple(there)

    def greet(self, barrier):
        for axis in range(2):
            for step in (-1, 1):
                @pl.when(self.has(axis, step))
                def _():
                    pl.semaphore_signal(
                        barrier, inc=1, device_id=self.partner(axis, step), device_id_type=MESH
                    )

    def met(self, barrier):
        partners = [self.has(axis, step).astype(jnp.int32) for axis in range(2) for step in (-1, 1)]
        pl.semaphore_wait(barrier, sum(partners))

    def send(self, source, target, axis, step, number):
        copy = pltpu.make_async_remote_copy(
            src_ref=source,
            dst_ref=target,
            send_sem=self.send_sems.at[number],
            recv_sem=self.recv_sems.at[number],
            device_id=self.partner(axis, step),
            device_id_type=MESH,
        )

        @pl.when(self.has(axis, step))
        def _():
            copy.start()

        self.copies.append((copy, axis, step))

    def finish(self):
        for copy, axis, step in self.copies:
            @pl.when(self.has(axis, step))
            def _():
                copy.wait_send()

            @pl.when(self.has(axis, -step))
            def _():
                copy.wait_recv()

        self.copies = []


def split(value):
    high = value.astype(jnp.bfloat16).astype(F32)
    return high, value - high


def dot_t(a, b):
    return lax.dot_general(
        a.astype(jnp.bfloat16),
        b.astype(jnp.bfloat16),
        (((1,), (1,)), ((), ())),
        preferred_element_type=F32,
    )


def pack(traces, owner, cell, resample, devices):
    held = traces.shape[0]
    owner_row = owner[...]
    cell_row = cell[...]
    member = lax.broadcasted_iota(jnp.int32, (devices, held), 0) == owner_row
    member = jnp.where(member, 1.0, 0.0)
    earlier = lax.broadcasted_iota(jnp.int32, (LANES, LANES), 0) < lax.broadcasted_iota(
        jnp.int32, (LANES, LANES), 1
    )
    earlier = jnp.where(earlier, 1.0, 0.0).astype(jnp.bfloat16)
    running = jnp.zeros((devices, 1), F32)
    position = []
    for block in range(held // LANES):
        part = member[:, block * LANES : (block + 1) * LANES]
        before = jnp.dot(part.astype(jnp.bfloat16), earlier, preferred_element_type=F32) + running
        position.append(jnp.sum(part * before, axis=0, keepdims=True))
        running = running + jnp.sum(part, axis=1, keepdims=True)
    position = jnp.concatenate(position, axis=1).astype(jnp.int32)

    steps = resample.shape[0]
    filt = jnp.concatenate([resample[...], jnp.zeros((SLOT - steps, resample.shape[1]), F32)], 0)
    filt_high, filt_low = split(filt)
    trace_high, trace_low = split(traces[...])
    both = dot_t(jnp.concatenate([filt_high, filt_low], 0), trace_high)
    fields = both[:SLOT] + both[SLOT:] + dot_t(filt_high, trace_low)
    kind = lax.broadcasted_iota(jnp.int32, (SLOT, held), 0)
    fields = jnp.where(kind == steps, (cell_row // LANES).astype(F32), fields)
    fields = jnp.where(kind == steps + 1, (cell_row % LANES).astype(F32), fields)
    first, rest = split(fields)
    second, third = split(rest)
    packed = []
    for piece in (third, second, first):
        spread = [
            jnp.where(position == q, piece, 0.0) for q in range(LANES // SLOT)
        ]
        packed.append(dot_t(member, jnp.concatenate(spread, 0)))
    return (packed[0] + packed[1]) + packed[2]


def route(
    p_hbm, vi_hbm, vx_hbm, vd_hbm, m_hbm, b_hbm, traces_hbm, owner_hbm, cell_hbm, resample_hbm,
    p, vi, vx, vd, modulus, buoyancy, ghost_i, ghost_x, ghost_bi, ghost_bx, index, values, injected,
    outbox, inbox, behind_i, ahead_i, behind_x, ahead_x, from_vi, from_bi, from_vx, from_bx,
    first_x, last_x, last_vx, last_bx,
    traces, owner, cell, resample,
    load_sems, node_sems, send_sems, recv_sems, post_sem, mail_sem,
):
    devices = lax.axis_size("xline") * lax.axis_size("inline")
    lines = lax.axis_size("inline")
    planes, tiles = p.shape[0], p.shape[1] // SUBLANES
    loads = [
        pltpu.make_async_copy(source, target, load_sems.at[k])
        for k, (source, target) in enumerate(
            ((p_hbm, p), (b_hbm, buoyancy), (vi_hbm, vi), (vx_hbm, vx), (vd_hbm, vd), (m_hbm, modulus))
        )
    ]
    node_loads = [
        pltpu.make_async_copy(source, target, node_sems.at[k])
        for k, (source, target) in enumerate(
            ((owner_hbm, owner), (cell_hbm, cell.at[0]), (resample_hbm, resample), (traces_hbm, traces))
        )
    ]
    for load in node_loads + loads:
        load.start()
    barrier = pltpu.get_barrier_semaphore()
    me = lax.axis_index("xline") * lines + lax.axis_index("inline")

    def other(k):
        there = lax.rem(me + k, devices)
        return there, (there // lines, lax.rem(there, lines))

    def greet(k, _):
        pl.semaphore_signal(barrier, inc=1, device_id=other(k)[1], device_id_type=MESH)
        return _

    lax.fori_loop(1, devices, greet, 0)

    for load in node_loads:
        load.wait()
    packed = pack(traces, owner, cell, resample, devices)
    for row in range(devices):
        outbox[row] = packed[row : row + 1]
    inbox[me] = outbox[me]

    pl.semaphore_wait(barrier, devices - 1)

    def post(k, _):
        there, device = other(k)
        pltpu.make_async_remote_copy(
            src_ref=outbox.at[there],
            dst_ref=inbox.at[me],
            send_sem=post_sem,
            recv_sem=mail_sem,
            device_id=device,
            device_id_type=MESH,
        ).start()
        return _

    lax.fori_loop(1, devices, post, 0)

    halo = Exchange(send_sems, recv_sems)
    for ref in (behind_i, from_vi, from_bi):
        @pl.when(jnp.logical_not(halo.has(1, -1)))
        def _():
            ref[...] = jnp.zeros_like(ref)
    for ref in (behind_x, from_vx, from_bx):
        @pl.when(jnp.logical_not(halo.has(0, -1)))
        def _():
            ref[...] = jnp.zeros_like(ref)

    @pl.when(jnp.logical_not(halo.has(1, 1)))
    def _():
        ahead_i[...] = jnp.zeros_like(ahead_i)

    @pl.when(jnp.logical_not(halo.has(0, 1)))
    def _():
        ahead_x[...] = jnp.zeros_like(ahead_x)

    loads[0].wait()
    halo.send(p.at[planes - 1], behind_i, 1, 1, 0)
    halo.send(p.at[0], ahead_i, 1, -1, 1)
    take_row(p, 0, first_x)
    halo.send(first_x, ahead_x, 0, -1, 2)
    take_row(p, p.shape[1] - 1, last_x)
    halo.send(last_x, behind_x, 0, 1, 3)
    loads[1].wait()
    halo.send(buoyancy.at[planes - 1], from_bi, 1, 1, 4)
    take_row(buoyancy, p.shape[1] - 1, last_bx)
    halo.send(last_bx, from_bx, 0, 1, 5)
    loads[2].wait()
    halo.send(vi.at[planes - 1], from_vi, 1, 1, 6)
    loads[3].wait()
    take_row(vx, p.shape[1] - 1, last_vx)
    halo.send(last_vx, from_vx, 0, 1, 7)
    loads[4].wait()
    loads[5].wait()

    v = (vi, vx, vd)
    velocity_inside(p, v, v, buoyancy)

    def clear(k, _):
        injected[pl.ds(pl.multiple_of(k * 64, 64), 64), :] = jnp.zeros((64, LANES), F32)
        return _

    lax.fori_loop(0, injected.shape[0] // 64, clear, 0)

    halo.finish()
    velocity_edge(p, v, v, buoyancy, ahead_i, ahead_x)
    ghosts(p, first_x, behind_i, behind_x, (from_vi, from_vx), (ghost_i, ghost_x), (from_bi, from_bx))
    ghost_bi[...] = from_bi[...]
    ghost_bx[...] = from_bx[...]

    def strip(i, tile, first):
        pressure(p, p, v, (ghost_i, ghost_x), modulus, i, tile, first, None)

    shell(planes, tiles, strip)
    core(planes, tiles, strip)

    mail = pltpu.make_async_remote_copy(
        src_ref=outbox.at[pl.ds(0, devices - 1)],
        dst_ref=inbox.at[pl.ds(0, devices - 1)],
        send_sem=post_sem,
        recv_sem=mail_sem,
        device_id=other(1)[1],
        device_id_type=MESH,
    )
    mail.wait_send()
    mail.wait_recv()
    arrived = inbox[...].reshape(devices, LANES)
    index[...] = arrived.astype(jnp.int32)
    values[...] = arrived.T


def scatter(index_ref, values, _, injected, index, sem):
    load = pltpu.make_async_copy(index_ref, index, sem)
    load.start()
    load.wait()
    devices = index.shape[0]
    lane = lax.broadcasted_iota(jnp.int32, (STEPS, LANES), 1)
    group = 3

    def sender(d, carry):
        pick = jnp.full((SUBLANES, LANES), d, jnp.int32)
        for start in range(0, 15, group):
            tiles, adds = [], []
            for q in range(start, start + group):
                tile = index[d, q * SLOT + STEPS]
                depth = index[d, q * SLOT + STEPS + 1]
                value = jnp.take_along_axis(values[pl.ds(q * SLOT, SLOT), :], pick, axis=1)[:STEPS]
                tiles.append(tile)
                adds.append(jnp.where(lane == depth, value, 0.0))
            spots = [pl.ds(pl.multiple_of(tile * STEPS, STEPS), STEPS) for tile in tiles]
            old = [injected[spot, :] for spot in spots]
            for b in range(group):
                new = old[b] + adds[b]
                for a in range(b):
                    new = new + jnp.where(tiles[a] == tiles[b], adds[a], 0.0)
                injected[spots[b], :] = new
        return carry

    lax.fori_loop(0, devices, sender, 0)


def advance(
    p_in, vi_in, vx_in, vd_in, modulus, buoyancy, ghost_i_in, ghost_x_in, ghost_bi, ghost_bx, injected,
    p, vi, vx, vd,
    ghost_i, ghost_x, behind_i, ahead_i, behind_x, ahead_x, first_x, last_x, send_sems, recv_sems,
):
    planes, tiles = p.shape[0], p.shape[1] // SUBLANES
    halo = Exchange(None, None)
    barrier = pltpu.get_barrier_semaphore()
    halo.greet(barrier)

    @pl.when(jnp.logical_not(halo.has(1, -1)))
    def _():
        behind_i[...] = jnp.zeros_like(behind_i)

    @pl.when(jnp.logical_not(halo.has(0, -1)))
    def _():
        behind_x[...] = jnp.zeros_like(behind_x)

    @pl.when(jnp.logical_not(halo.has(1, 1)))
    def _():
        ahead_i[...] = jnp.zeros_like(ahead_i)

    @pl.when(jnp.logical_not(halo.has(0, 1)))
    def _():
        ahead_x[...] = jnp.zeros_like(ahead_x)

    def source(step):
        def strip(i, tile, h):
            row = ((i * p.shape[1] + tile * SUBLANES) * 2 + h) * STEPS + step
            return injected[pl.ds(row, SUBLANES, stride=2 * STEPS), :]

        return strip

    def send(step):
        halo.send_sems, halo.recv_sems = send_sems.at[step], recv_sems.at[step]
        halo.send(p.at[planes - 1], behind_i.at[step], 1, 1, 0)
        halo.send(p.at[0], ahead_i.at[step], 1, -1, 1)
        take_row(p, 0, first_x.at[step])
        halo.send(first_x.at[step], ahead_x.at[step], 0, -1, 2)
        take_row(p, p.shape[1] - 1, last_x.at[step])
        halo.send(last_x.at[step], behind_x.at[step], 0, 1, 3)

    def inject(i, tile, first):
        del first
        spread = source(0)
        for h in range(2):
            at = (i, rows(tile), cols(h))
            p[at] = p_in[at] + COURANT * modulus[at] * spread(i, tile, h)

    shell(planes, tiles, inject)
    halo.met(barrier)
    send(0)
    core(planes, tiles, inject)

    v = (vi, vx, vd)
    for step in range(1, STEPS):
        v_in = (vi_in, vx_in, vd_in) if step == 1 else v
        ghost_in = (ghost_i_in, ghost_x_in) if step == 1 else (ghost_i, ghost_x)
        velocity_inside(p, v_in, v, buoyancy)
        halo.finish()
        velocity_edge(p, v_in, v, buoyancy, ahead_i.at[step - 1], ahead_x.at[step - 1])
        ghosts(
            p, first_x.at[step - 1], behind_i.at[step - 1], behind_x.at[step - 1],
            ghost_in, (ghost_i, ghost_x), (ghost_bi, ghost_bx),
        )

        def strip(i, tile, first):
            pressure(p, p, v, (ghost_i, ghost_x), modulus, i, tile, first, source(step))

        shell(planes, tiles, strip)
        if step < STEPS - 1:
            send(step)
        core(planes, tiles, strip)


def shards(
    pressure_in, vel_inline, vel_xline, vel_depth, modulus, buoyancy, traces, owner, node_cell, resample
):
    planes, wide, deep = pressure_in.shape
    devices = lax.axis_size("xline") * lax.axis_size("inline")
    held = traces.shape[0]
    field = (planes, wide, deep)
    plane, column = (wide, deep), (2, planes, LANES)
    injection = (planes * wide * deep // LANES * STEPS, LANES)
    vmem = pl.BlockSpec(memory_space=VMEM)
    hbm = pl.BlockSpec(memory_space=HBM)
    dma = pltpu.SemaphoreType.DMA

    state = pl.pallas_call(
        route,
        out_shape=[VMEM(field, F32)] * 6
        + [VMEM(plane, F32), VMEM(column, F32)] * 2
        + [VMEM((devices, LANES), jnp.int32), VMEM((LANES, devices), F32), VMEM(injection, F32)],
        in_specs=[hbm] * 10,
        out_specs=[vmem] * 13,
        scratch_shapes=[VMEM((devices, 1, LANES), F32)] * 2
        + [VMEM(plane, F32)] * 2
        + [VMEM(column, F32)] * 2
        + [VMEM(plane, F32)] * 2
        + [VMEM(column, F32)] * 6
        + [
            VMEM(traces.shape, F32), VMEM((1, held), jnp.int32), VMEM((1, held), jnp.int32),
            VMEM(resample.shape, F32),
        ]
        + [dma((6,)), dma((4,)), dma((8,)), dma((8,)), dma, dma],
        compiler_params=pltpu.CompilerParams(collective_id=0, has_side_effects=True, vmem_limit_bytes=16 * 2**20),
        name="route",
    )(
        *(
            pltpu.with_memory_space_constraint(x, HBM)
            for x in (
                pressure_in, vel_inline, vel_xline, vel_depth, modulus, buoyancy,
                traces, owner.reshape(1, held), node_cell, resample,
            )
        )
    )
    *fields, index, values, cleared = state
    injected = pl.pallas_call(
        scatter,
        out_shape=VMEM(injection, F32),
        in_specs=[vmem] * 3,
        out_specs=vmem,
        scratch_shapes=[pltpu.SMEM((devices, LANES), jnp.int32), dma],
        input_output_aliases={2: 0},
        compiler_params=pltpu.CompilerParams(vmem_limit_bytes=16 * 2**20),
        name="scatter",
    )(index, values, cleared)
    rounds = STEPS - 1
    return pl.pallas_call(
        advance,
        out_shape=[VMEM(field, F32)] * 4,
        in_specs=[vmem] * 11,
        out_specs=[vmem] * 4,
        scratch_shapes=[VMEM(plane, F32), VMEM(column, F32)]
        + [VMEM((rounds, *plane), F32)] * 2
        + [VMEM((rounds, *column), F32)] * 4
        + [dma((rounds, 4)), dma((rounds, 4))],
        compiler_params=pltpu.CompilerParams(collective_id=1, has_side_effects=True, vmem_limit_bytes=16 * 2**20),
        name="advance",
    )(*fields, injected)


def solution(mesh):
    field = P("inline", "xline", None)
    nodes = ("xline", "inline")
    return jax.shard_map(
        shards,
        mesh=mesh,
        in_specs=(field,) * 6 + (P(nodes, None), P(nodes, None), P(nodes), P()),
        out_specs=(field,) * 4,
        check_vma=False,
    )
```

profile of v0, /device:TPU:8, one launch (start us, length us, event | category | flops | bytes accessed | tf_op | source)
XLA Modules:
  0.0 67.4 jit_solution(10671058212834423774)
XLA Ops:
  0.6 21.0 %route.1 = (f32[32,64,256]{2,1,0:T(8,128)S(1)}, f32[32,64,256]{2,1,0:T(8,128)S(1)}, f32[32,64,256]{2,1,0:T(8,128)S(1)}, f32[32,64,256]{2,1,0:T(8,128)S(1)}, f32[...) custom-call(f32[32,64,256]{2,1,0:T(8,128)} %p_hbm.1, ...), custom_call_target="tpu_custom_call" | custom-call | tf_op jit(solution)/shard_map/route/pallas_call | solution.py:515
  21.7 16.2 %scatter.1.injected = f32[16384,128]{1,0:T(8,128)S(1)} custom-call(s32[128,128]{1,0:T(8,128)S(1)} %get-tuple-element.27.index_ref, f32[128,128]{1,0:T(8,128)S(1)} %get-tuple-element.28.values, f32[16384,128]{1,0:T(8,128)S(1)} %get-tuple-element.29._), custom_call_target="tpu_custom_call", output_to_operand_aliasing={{}: (2, {})} | custom-call | tf_op jit(solution)/shard_map/scatter/pallas_call | solution.py:544
  37.9 24.2 %advance.1 = (f32[32,64,256]{2,1,0:T(8,128)S(1)}, f32[32,64,256]{2,1,0:T(8,128)S(1)}, f32[32,64,256]{2,1,0:T(8,128)S(1)}, f32[32,64,256]{2,1,0:T(8,128)S(1)}) custom-call(f32[32,64,256]{2,1,0:T(8,128)S(1)} %get-tuple-element.17.p_in, f32[32,64,256]{2,1,0:T(8,128)S(1)} %get-tuple-element.18.vi_in, f32[32,64,256]{2,1,0:T(8,128)S(1)} %get-tuple-element.19.vx_in, ...), custom_call_target="tpu_custom_call" | custom-call | tf_op jit(solution)/shard_map/advance/pallas_call | solution.py:555
  62.1 1.3 %copy.20 = f32[32,64,256]{2,1,0:T(8,128)} copy(f32[32,64,256]{2,1,0:T(8,128)S(1)} %get-tuple-element.30) | data formatting | bytes 4194304
  63.5 1.3 %copy.21 = f32[32,64,256]{2,1,0:T(8,128)} copy(f32[32,64,256]{2,1,0:T(8,128)S(1)} %get-tuple-element.31) | data formatting | bytes 4194304
  64.8 1.3 %copy.22 = f32[32,64,256]{2,1,0:T(8,128)} copy(f32[32,64,256]{2,1,0:T(8,128)S(1)} %get-tuple-element.32) | data formatting | bytes 4194304
  66.1 1.3 %copy.23 = f32[32,64,256]{2,1,0:T(8,128)} copy(f32[32,64,256]{2,1,0:T(8,128)S(1)} %get-tuple-element.33) | data formatting | bytes 4194304
where the time goes:
time: 67.5 us; the launch traced here: 67.4 us
  Pallas kernels  61.5 us (91%)
  local copies, waits for them, and re-layouts  5.28 us (8%)
    pallas_call x1, Pallas kernels, shards(): pl.pallas_call(advance, out_shape=[VMEM(field, F32)] * 4, in_specs=[vmem]...  24.2 us
    pallas_call x1, Pallas kernels, shards(): pl.pallas_call(route, out_shape=[VMEM(field, F32)] * 6 + [VMEM(plane, F32...  21 us
    pallas_call x1, Pallas kernels, shards(): pl.pallas_call(scatter, out_shape=VMEM(injection, F32), in_specs=[vmem] *...  16.2 us
    unnamed x4, local copies, waits for them, and re-layouts  5.28 us

commit v1 on v0

--- a/solution.py
+++ b/solution.py
@@ -13,6 +13,7 @@
 MESH = pl.DeviceIdType.MESH
 VMEM, HBM = pltpu.MemorySpace.VMEM, pltpu.MemorySpace.HBM
 F32 = jnp.float32
+LIMIT = 16 * 2**20
 
 
 def lane_ids():
@@ -57,7 +58,7 @@
             velocity(p, v_in, v_out, buoyancy, i, tile, True)
         return _
 
-    lax.fori_loop(0, planes - 1, plane, 0)
+    lax.fori_loop(0, planes - 1, plane, 0, unroll=6)
     for tile in range(tiles):
         velocity(p, v_in, v_out, buoyancy, planes - 1, tile, False)
 
@@ -85,7 +86,7 @@
             vx_out[at] = vx[at] - COURANT * buoyancy[at] * (ahead - here)
         return _
 
-    lax.fori_loop(0, planes, plane, 0, unroll=4)
+    lax.fori_loop(0, planes, plane, 0, unroll=16)
 
 
 def ghosts(p, first_x, behind_i, behind_x, ghost_in, ghost_out, ghost_b):
@@ -119,6 +120,14 @@
         p_out[at] = p_in[at] - COURANT * modulus[at] * total
 
 
+def source(injected, wide, step):
+    def strip(i, tile, h):
+        row = ((i * wide + tile * SUBLANES) * 2 + h) * STEPS + step
+        return injected[pl.ds(row, SUBLANES, stride=2 * STEPS), :]
+
+    return strip
+
+
 def shell(planes, tiles, strip):
     for tile in range(tiles):
         strip(0, tile, True)
@@ -129,7 +138,7 @@
         strip(i, tiles - 1, False)
         return _
 
-    lax.fori_loop(1, planes - 1, plane, 0, unroll=2)
+    lax.fori_loop(1, planes - 1, plane, 0, unroll=15)
 
 
 def core(planes, tiles, strip):
@@ -138,7 +147,7 @@
             strip(i, tile, False)
         return _
 
-    lax.fori_loop(1, planes - 1, plane, 0)
+    lax.fori_loop(1, planes - 1, plane, 0, unroll=6)
 
 
 def take_row(source, row, target):
@@ -147,7 +156,7 @@
             target[h, pl.ds(i, 1), :] = source[i, pl.ds(row, 1), cols(h)]
         return _
 
-    lax.fori_loop(0, source.shape[0], plane, 0, unroll=8)
+    lax.fori_loop(0, source.shape[0], plane, 0, unroll=16)
 
 
 class Exchange:
@@ -247,8 +256,7 @@
     both = dot_t(jnp.concatenate([filt_high, filt_low], 0), trace_high)
     fields = both[:SLOT] + both[SLOT:] + dot_t(filt_high, trace_low)
     kind = lax.broadcasted_iota(jnp.int32, (SLOT, held), 0)
-    fields = jnp.where(kind == steps, (cell_row // LANES).astype(F32), fields)
-    fields = jnp.where(kind == steps + 1, (cell_row % LANES).astype(F32), fields)
+    fields = jnp.where(kind == steps, cell_row.astype(F32), fields)
     first, rest = split(fields)
     second, third = split(rest)
     packed = []
@@ -389,29 +397,32 @@
     )
     mail.wait_send()
     mail.wait_recv()
-    arrived = inbox[...].reshape(devices, LANES)
-    index[...] = arrived.astype(jnp.int32)
-    values[...] = arrived.T
+    values[...] = inbox[...].reshape(devices, LANES).T
+    index[...] = values[pl.ds(STEPS, LANES // SLOT, stride=SLOT), :].astype(jnp.int32)
 
 
 def scatter(index_ref, values, _, injected, index, sem):
     load = pltpu.make_async_copy(index_ref, index, sem)
     load.start()
-    load.wait()
-    devices = index.shape[0]
+    devices = values.shape[1]
     lane = lax.broadcasted_iota(jnp.int32, (STEPS, LANES), 1)
-    group = 3
-
-    def sender(d, carry):
+    slots, group = 15, 3
+
+    def spread(d):
         pick = jnp.full((SUBLANES, LANES), d, jnp.int32)
-        for start in range(0, 15, group):
+        return [
+            jnp.take_along_axis(values[pl.ds(q * SLOT, SLOT), :], pick, axis=1)[:STEPS]
+            for q in range(slots)
+        ]
+
+    def sender(d, now):
+        later = spread(jnp.minimum(d + 1, devices - 1))
+        for start in range(0, slots, group):
             tiles, adds = [], []
             for q in range(start, start + group):
-                tile = index[d, q * SLOT + STEPS]
-                depth = index[d, q * SLOT + STEPS + 1]
-                value = jnp.take_along_axis(values[pl.ds(q * SLOT, SLOT), :], pick, axis=1)[:STEPS]
-                tiles.append(tile)
-                adds.append(jnp.where(lane == depth, value, 0.0))
+                cell = index[q, d]
+                tiles.append(lax.shift_right_logical(cell, 7))
+                adds.append(jnp.where(lane == (cell & (LANES - 1)), now[q], 0.0))
             spots = [pl.ds(pl.multiple_of(tile * STEPS, STEPS), STEPS) for tile in tiles]
             old = [injected[spot, :] for spot in spots]
             for b in range(group):
@@ -419,15 +430,17 @@
                 for a in range(b):
                     new = new + jnp.where(tiles[a] == tiles[b], adds[a], 0.0)
                 injected[spots[b], :] = new
-        return carry
-
-    lax.fori_loop(0, devices, sender, 0)
+        return later
+
+    first = spread(0)
+    load.wait()
+    lax.fori_loop(0, devices, sender, first, unroll=4)
 
 
 def advance(
     p_in, vi_in, vx_in, vd_in, modulus, buoyancy, ghost_i_in, ghost_x_in, ghost_bi, ghost_bx, injected,
-    p, vi, vx, vd,
-    ghost_i, ghost_x, behind_i, ahead_i, behind_x, ahead_x, first_x, last_x, send_sems, recv_sems,
+    p, vi, vx, vd, ghost_i, ghost_x,
+    behind_i, ahead_i, behind_x, ahead_x, first_x, last_x, send_sems, recv_sems,
 ):
     planes, tiles = p.shape[0], p.shape[1] // SUBLANES
     halo = Exchange(None, None)
@@ -449,13 +462,6 @@
     @pl.when(jnp.logical_not(halo.has(0, 1)))
     def _():
         ahead_x[...] = jnp.zeros_like(ahead_x)
-
-    def source(step):
-        def strip(i, tile, h):
-            row = ((i * p.shape[1] + tile * SUBLANES) * 2 + h) * STEPS + step
-            return injected[pl.ds(row, SUBLANES, stride=2 * STEPS), :]
-
-        return strip
 
     def send(step):
         halo.send_sems, halo.recv_sems = send_sems.at[step], recv_sems.at[step]
@@ -468,7 +474,7 @@
 
     def inject(i, tile, first):
         del first
-        spread = source(0)
+        spread = source(injected, p.shape[1], 0)
         for h in range(2):
             at = (i, rows(tile), cols(h))
             p[at] = p_in[at] + COURANT * modulus[at] * spread(i, tile, h)
@@ -490,13 +496,51 @@
             ghost_in, (ghost_i, ghost_x), (ghost_bi, ghost_bx),
         )
 
+        if step == STEPS - 1:
+            break
+        spread = source(injected, p.shape[1], step)
+
         def strip(i, tile, first):
-            pressure(p, p, v, (ghost_i, ghost_x), modulus, i, tile, first, source(step))
+            pressure(p, p, v, (ghost_i, ghost_x), modulus, i, tile, first, spread)
 
         shell(planes, tiles, strip)
-        if step < STEPS - 1:
-            send(step)
+        send(step)
         core(planes, tiles, strip)
+
+
+def finish(
+    p_in, vi, vx, vd, ghost_i, ghost_x, modulus, injected,
+    p_out, vi_out, vx_out, vd_out,
+    p, sems,
+):
+    planes, tiles = p_in.shape[0], p_in.shape[1] // SUBLANES
+    copies = [
+        pltpu.make_async_copy(source, target, sems.at[k])
+        for k, (source, target) in enumerate(((vi, vi_out), (vx, vx_out), (vd, vd_out)))
+    ]
+    for copy in copies:
+        copy.start()
+    spread = source(injected, p_in.shape[1], STEPS - 1)
+    v, ghost = (vi, vx, vd), (ghost_i, ghost_x)
+    chunks = 4
+    size = planes // chunks
+
+    def plane(i, _):
+        for tile in range(tiles):
+            pressure(p_in, p, v, ghost, modulus, i, tile, False, spread)
+        return _
+
+    for chunk in range(chunks):
+        start = chunk * size
+        if chunk == 0:
+            for tile in range(tiles):
+                pressure(p_in, p, v, ghost, modulus, 0, tile, True, spread)
+        lax.fori_loop(max(start, 1), start + size, plane, 0, unroll=size if chunk else size - 1)
+        part = pl.ds(start, size)
+        copies.append(pltpu.make_async_copy(p.at[part], p_out.at[part], sems.at[3 + chunk]))
+        copies[-1].start()
+    for copy in copies:
+        copy.wait()
 
 
 def shards(
@@ -516,7 +560,7 @@
         route,
         out_shape=[VMEM(field, F32)] * 6
         + [VMEM(plane, F32), VMEM(column, F32)] * 2
-        + [VMEM((devices, LANES), jnp.int32), VMEM((LANES, devices), F32), VMEM(injection, F32)],
+        + [VMEM((LANES // SLOT, devices), jnp.int32), VMEM((LANES, devices), F32), VMEM(injection, F32)],
         in_specs=[hbm] * 10,
         out_specs=[vmem] * 13,
         scratch_shapes=[VMEM((devices, 1, LANES), F32)] * 2
@@ -529,7 +573,7 @@
             VMEM(resample.shape, F32),
         ]
         + [dma((6,)), dma((4,)), dma((8,)), dma((8,)), dma, dma],
-        compiler_params=pltpu.CompilerParams(collective_id=0, has_side_effects=True, vmem_limit_bytes=16 * 2**20),
+        compiler_params=pltpu.CompilerParams(collective_id=0, has_side_effects=True, vmem_limit_bytes=LIMIT),
         name="route",
     )(
         *(
@@ -546,24 +590,35 @@
         out_shape=VMEM(injection, F32),
         in_specs=[vmem] * 3,
         out_specs=vmem,
-        scratch_shapes=[pltpu.SMEM((devices, LANES), jnp.int32), dma],
+        scratch_shapes=[pltpu.SMEM((LANES // SLOT, devices), jnp.int32), dma],
         input_output_aliases={2: 0},
-        compiler_params=pltpu.CompilerParams(vmem_limit_bytes=16 * 2**20),
+        compiler_params=pltpu.CompilerParams(vmem_limit_bytes=LIMIT),
         name="scatter",
     )(index, values, cleared)
     rounds = STEPS - 1
-    return pl.pallas_call(
+    *fields, ghost_i, ghost_x = pl.pallas_call(
         advance,
-        out_shape=[VMEM(field, F32)] * 4,
+        out_shape=[VMEM(field, F32)] * 4 + [VMEM(plane, F32), VMEM(column, F32)],
         in_specs=[vmem] * 11,
-        out_specs=[vmem] * 4,
-        scratch_shapes=[VMEM(plane, F32), VMEM(column, F32)]
-        + [VMEM((rounds, *plane), F32)] * 2
+        out_specs=[vmem] * 6,
+        scratch_shapes=[VMEM((rounds, *plane), F32)] * 2
         + [VMEM((rounds, *column), F32)] * 4
         + [dma((rounds, 4)), dma((rounds, 4))],
-        compiler_params=pltpu.CompilerParams(collective_id=1, has_side_effects=True, vmem_limit_bytes=16 * 2**20),
+        compiler_params=pltpu.CompilerParams(
+            collective_id=1, has_side_effects=True, vmem_limit_bytes=LIMIT
+        ),
         name="advance",
     )(*fields, injected)
+    modulus = state[4]
+    return pl.pallas_call(
+        finish,
+        out_shape=[HBM(field, F32)] * 4,
+        in_specs=[vmem] * 8,
+        out_specs=[hbm] * 4,
+        scratch_shapes=[VMEM(field, F32), dma((7,))],
+        compiler_params=pltpu.CompilerParams(vmem_limit_bytes=LIMIT),
+        name="finish",
+    )(*fields, ghost_i, ghost_x, modulus, injected)
 
 
 def solution(mesh):

time: 67.5 us -> 45.2 us (0.67)
  Pallas kernels: 61.5 us -> 44.4 us
  local copies, waits for them, and re-layouts: 5.28 us -> 0 us
    pallas_call x1, Pallas kernels: 16.2 us -> 7.27 us  [shards(): pl.pallas_call(scatter, out_shape=VMEM(injection, F32), in_specs=[vmem] *...]
    pallas_call x1 -> x2, Pallas kernels: 24.2 us -> 18.5 us  [the longest x1 15.2 us: shards(): pl.pallas_call(advance, out_shape=[VMEM(field, F32)] * 4 + [VMEM(plane, F...]
    unnamed x4 -> x0, local copies, waits for them, and re-layouts: 5.28 us -> none
    pallas_call x1, Pallas kernels: 21 us -> 18.6 us  [shards(): pl.pallas_call(route, out_shape=[VMEM(field, F32)] * 6 + [VMEM(plane, F32...]
where the time goes in v1:
time: 45.2 us; the launch traced here: 45.1 us
  Pallas kernels  44.4 us (98%)
  between operations  0.66 us (1%)
    pallas_call x1, Pallas kernels, shards(): pl.pallas_call(route, out_shape=[VMEM(field, F32)] * 6 + [VMEM(plane, F32...  18.6 us
    pallas_call x1, Pallas kernels, shards(): pl.pallas_call(advance, out_shape=[VMEM(field, F32)] * 4 + [VMEM(plane, F...  15.2 us
    pallas_call x1, Pallas kernels, shards(): pl.pallas_call(scatter, out_shape=VMEM(injection, F32), in_specs=[vmem] *...  7.27 us
    pallas_call x1, Pallas kernels, shards(): pl.pallas_call(finish, out_shape=[HBM(field, F32)] * 4, in_specs=[vmem] *...  3.34 us

profile of v1, /device:TPU:8, one launch (start us, length us, event | category | flops | bytes accessed | tf_op | source)
XLA Modules:
  0.0 45.1 jit_solution(835051058897300022)
XLA Ops:
  0.6 18.6 %route.1 = (f32[32,64,256]{2,1,0:T(8,128)S(1)}, f32[32,64,256]{2,1,0:T(8,128)S(1)}, f32[32,64,256]{2,1,0:T(8,128)S(1)}, f32[32,64,256]{2,1,0:T(8,128)S(1)}, f32[...) custom-call(f32[32,64,256]{2,1,0:T(8,128)} %p_hbm.1, ...), custom_call_target="tpu_custom_call" | custom-call | tf_op jit(solution)/shard_map/route/pallas_call | solution.py:559
  19.2 7.3 %scatter.1.injected = f32[16384,128]{1,0:T(8,128)S(1)} custom-call(s32[16,128]{1,0:T(8,128)S(1)} %get-tuple-element.33.index_ref, f32[128,128]{1,0:T(8,128)S(1)} %get-tuple-element.34.values, f32[16384,128]{1,0:T(8,128)S(1)} %get-tuple-element.35._), custom_call_target="tpu_custom_call", output_to_operand_aliasing={{}: (2, {})} | custom-call | tf_op jit(solution)/shard_map/scatter/pallas_call | solution.py:588
  26.5 15.2 %advance.1 = (f32[32,64,256]{2,1,0:T(8,128)S(1)}, f32[32,64,256]{2,1,0:T(8,128)S(1)}, f32[32,64,256]{2,1,0:T(8,128)S(1)}, f32[32,64,256]{2,1,0:T(8,128)S(1)}, f3...) custom-call(f32[32,64,256]{2,1,0:T(8,128)S(1)} %get-tuple-element.23.p_in, f32[32,64,256]{2,1,0:T(8,128)S(1)} %get-tuple-element.24.vi_in, ...), custom_call_target="tpu_custom_call" | custom-call | tf_op jit(solution)/shard_map/advance/pallas_call | solution.py:599
  41.7 3.3 %finish.1 = (f32[32,64,256]{2,1,0:T(8,128)}, f32[32,64,256]{2,1,0:T(8,128)}, f32[32,64,256]{2,1,0:T(8,128)}, f32[32,64,256]{2,1,0:T(8,128)}) custom-call(f32[32,64,256]{2,1,0:T(8,128)S(1)} %get-tuple-element.36.p_in, f32[32,64,256]{2,1,0:T(8,128)S(1)} %get-tuple-element.37.vi, f32[32,64,256]{2,1,0:T(8,128)S(1)} %get-tuple-element.38.vx, ...), custom_call_target="tpu_custom_call" | custom-call | tf_op jit(solution)/shard_map/finish/pallas_call | solution.py:613

commit v2 on v1

--- a/solution.py
+++ b/solution.py
@@ -10,6 +10,7 @@
 LANES = 128
 SUBLANES = 8
 SLOT = 8
+NEAR = 8
 MESH = pl.DeviceIdType.MESH
 VMEM, HBM = pltpu.MemorySpace.VMEM, pltpu.MemorySpace.HBM
 F32 = jnp.float32
@@ -271,10 +272,10 @@
 def route(
     p_hbm, vi_hbm, vx_hbm, vd_hbm, m_hbm, b_hbm, traces_hbm, owner_hbm, cell_hbm, resample_hbm,
     p, vi, vx, vd, modulus, buoyancy, ghost_i, ghost_x, ghost_bi, ghost_bx, index, values, injected,
-    outbox, inbox, behind_i, ahead_i, behind_x, ahead_x, from_vi, from_bi, from_vx, from_bx,
+    outbox, relay, inbox, behind_i, ahead_i, behind_x, ahead_x, from_vi, from_bi, from_vx, from_bx,
     first_x, last_x, last_vx, last_bx,
     traces, owner, cell, resample,
-    load_sems, node_sems, send_sems, recv_sems, post_sem, mail_sem,
+    load_sems, node_sems, send_sems, recv_sems, post_sems, mail_sems,
 ):
     devices = lax.axis_size("xline") * lax.axis_size("inline")
     lines = lax.axis_size("inline")
@@ -294,40 +295,64 @@
     for load in node_loads + loads:
         load.start()
     barrier = pltpu.get_barrier_semaphore()
-    me = lax.axis_index("xline") * lines + lax.axis_index("inline")
-
-    def other(k):
-        there = lax.rem(me + k, devices)
-        return there, (there // lines, lax.rem(there, lines))
-
-    def greet(k, _):
-        pl.semaphore_signal(barrier, inc=1, device_id=other(k)[1], device_id_type=MESH)
-        return _
-
-    lax.fori_loop(1, devices, greet, 0)
+    xline, inline = lax.axis_index("xline"), lax.axis_index("inline")
+    blocks = lines // NEAR
+    groups = devices // NEAR
+    group, near = xline * blocks + inline // NEAR, lax.rem(inline, NEAR)
+
+    def far_partner(k):
+        there = lax.rem(group + k, groups)
+        return there, (there // blocks, lax.rem(there, blocks) * NEAR + near)
+
+    def near_partner(k):
+        there = lax.rem(near + k, NEAR)
+        return there, (xline, inline - near + there)
+
+    def greet(device):
+        pl.semaphore_signal(barrier, inc=1, device_id=device, device_id_type=MESH)
+
+    def greet_far(k, _):
+        greet(far_partner(k)[1])
+        return _
+
+    def greet_near(k, _):
+        greet(near_partner(k)[1])
+        return _
+
+    lax.fori_loop(1, groups, greet_far, 0, unroll=True)
+    lax.fori_loop(1, NEAR, greet_near, 0, unroll=True)
+    crosses = []
+    for edge, step, end in ((NEAR - 1, 1, lines - 1), (0, -1, 0)):
+        cross = jnp.logical_and(near == edge, inline != end)
+        crosses.append(cross.astype(jnp.int32))
+
+        @pl.when(cross)
+        def _():
+            greet((xline, jnp.clip(inline + step, 0, lines - 1)))
 
     for load in node_loads:
         load.wait()
     packed = pack(traces, owner, cell, resample, devices)
     for row in range(devices):
         outbox[row] = packed[row : row + 1]
-    inbox[me] = outbox[me]
-
-    pl.semaphore_wait(barrier, devices - 1)
-
-    def post(k, _):
-        there, device = other(k)
+    for row in range(NEAR):
+        relay[row, group] = outbox[group * NEAR + row]
+
+    pl.semaphore_wait(barrier, groups - 1 + NEAR - 1 + sum(crosses))
+
+    def post_far(k, _):
+        there, device = far_partner(k)
         pltpu.make_async_remote_copy(
-            src_ref=outbox.at[there],
-            dst_ref=inbox.at[me],
-            send_sem=post_sem,
-            recv_sem=mail_sem,
+            src_ref=outbox.at[pl.ds(there * NEAR, NEAR)],
+            dst_ref=relay.at[:, group],
+            send_sem=post_sems.at[0],
+            recv_sem=mail_sems.at[0],
             device_id=device,
             device_id_type=MESH,
         ).start()
         return _
 
-    lax.fori_loop(1, devices, post, 0)
+    lax.fori_loop(1, groups, post_far, 0, unroll=True)
 
     halo = Exchange(send_sems, recv_sems)
     for ref in (behind_i, from_vi, from_bi):
@@ -369,6 +394,32 @@
     v = (vi, vx, vd)
     velocity_inside(p, v, v, buoyancy)
 
+    far_mail = pltpu.make_async_remote_copy(
+        src_ref=outbox.at[pl.ds(0, devices - NEAR)],
+        dst_ref=relay.at[:, pl.ds(0, groups - 1)],
+        send_sem=post_sems.at[0],
+        recv_sem=mail_sems.at[0],
+        device_id=far_partner(1)[1],
+        device_id_type=MESH,
+    )
+    far_mail.wait_send()
+    far_mail.wait_recv()
+
+    def post_near(k, _):
+        there, device = near_partner(k)
+        pltpu.make_async_remote_copy(
+            src_ref=relay.at[there],
+            dst_ref=inbox.at[near],
+            send_sem=post_sems.at[1],
+            recv_sem=mail_sems.at[1],
+            device_id=device,
+            device_id_type=MESH,
+        ).start()
+        return _
+
+    lax.fori_loop(1, NEAR, post_near, 0, unroll=True)
+    inbox[near] = relay[near]
+
     def clear(k, _):
         injected[pl.ds(pl.multiple_of(k * 64, 64), 64), :] = jnp.zeros((64, LANES), F32)
         return _
@@ -387,16 +438,16 @@
     shell(planes, tiles, strip)
     core(planes, tiles, strip)
 
-    mail = pltpu.make_async_remote_copy(
-        src_ref=outbox.at[pl.ds(0, devices - 1)],
-        dst_ref=inbox.at[pl.ds(0, devices - 1)],
-        send_sem=post_sem,
-        recv_sem=mail_sem,
-        device_id=other(1)[1],
+    near_mail = pltpu.make_async_remote_copy(
+        src_ref=relay.at[pl.ds(0, NEAR - 1)],
+        dst_ref=inbox.at[pl.ds(0, NEAR - 1)],
+        send_sem=post_sems.at[1],
+        recv_sem=mail_sems.at[1],
+        device_id=near_partner(1)[1],
         device_id_type=MESH,
     )
-    mail.wait_send()
-    mail.wait_recv()
+    near_mail.wait_send()
+    near_mail.wait_recv()
     values[...] = inbox[...].reshape(devices, LANES).T
     index[...] = values[pl.ds(STEPS, LANES // SLOT, stride=SLOT), :].astype(jnp.int32)
 
@@ -563,7 +614,8 @@
         + [VMEM((LANES // SLOT, devices), jnp.int32), VMEM((LANES, devices), F32), VMEM(injection, F32)],
         in_specs=[hbm] * 10,
         out_specs=[vmem] * 13,
-        scratch_shapes=[VMEM((devices, 1, LANES), F32)] * 2
+        scratch_shapes=[VMEM((devices, 1, LANES), F32)]
+        + [VMEM((NEAR, devices // NEAR, 1, LANES), F32)] * 2
         + [VMEM(plane, F32)] * 2
         + [VMEM(column, F32)] * 2
         + [VMEM(plane, F32)] * 2
@@ -572,7 +624,7 @@
             VMEM(traces.shape, F32), VMEM((1, held), jnp.int32), VMEM((1, held), jnp.int32),
             VMEM(resample.shape, F32),
         ]
-        + [dma((6,)), dma((4,)), dma((8,)), dma((8,)), dma, dma],
+        + [dma((6,)), dma((4,)), dma((8,)), dma((8,)), dma((2,)), dma((2,))],
         compiler_params=pltpu.CompilerParams(collective_id=0, has_side_effects=True, vmem_limit_bytes=LIMIT),
         name="route",
     )(

time: 45.2 us -> 44.8 us (level)
  no operation moved by 1% of the time
where the time goes in v2:
time: 44.8 us; the launch traced here: 44.7 us
  Pallas kernels  44.1 us (98%)
  between operations  0.66 us (1%)
    pallas_call x1, Pallas kernels, shards(): pl.pallas_call(route, out_shape=[VMEM(field, F32)] * 6 + [VMEM(plane, F32...  18.7 us
    pallas_call x1, Pallas kernels, shards(): pl.pallas_call(advance, out_shape=[VMEM(field, F32)] * 4 + [VMEM(plane, F...  15.2 us
    pallas_call x1, Pallas kernels, shards(): pl.pallas_call(scatter, out_shape=VMEM(injection, F32), in_specs=[vmem] *...  6.83 us
    pallas_call x1, Pallas kernels, shards(): pl.pallas_call(finish, out_shape=[HBM(field, F32)] * 4, in_specs=[vmem] *...  3.34 us

profile of v2, /device:TPU:8, one launch (start us, length us, event | category | flops | bytes accessed | tf_op | source)
XLA Modules:
  0.0 44.7 jit_solution(4423646262515569255)
XLA Ops:
  0.6 18.7 %route.1 = (f32[32,64,256]{2,1,0:T(8,128)S(1)}, f32[32,64,256]{2,1,0:T(8,128)S(1)}, f32[32,64,256]{2,1,0:T(8,128)S(1)}, f32[32,64,256]{2,1,0:T(8,128)S(1)}, f32[...) custom-call(f32[32,64,256]{2,1,0:T(8,128)} %p_hbm.1, ...), custom_call_target="tpu_custom_call" | custom-call | tf_op jit(solution)/shard_map/route/pallas_call | solution.py:610
  19.4 6.8 %scatter.1.injected = f32[16384,128]{1,0:T(8,128)S(1)} custom-call(s32[16,128]{1,0:T(8,128)S(1)} %get-tuple-element.33.index_ref, f32[128,128]{1,0:T(8,128)S(1)} %get-tuple-element.34.values, f32[16384,128]{1,0:T(8,128)S(1)} %get-tuple-element.35._), custom_call_target="tpu_custom_call", output_to_operand_aliasing={{}: (2, {})} | custom-call | tf_op jit(solution)/shard_map/scatter/pallas_call | solution.py:640
  26.2 15.2 %advance.1 = (f32[32,64,256]{2,1,0:T(8,128)S(1)}, f32[32,64,256]{2,1,0:T(8,128)S(1)}, f32[32,64,256]{2,1,0:T(8,128)S(1)}, f32[32,64,256]{2,1,0:T(8,128)S(1)}, f3...) custom-call(f32[32,64,256]{2,1,0:T(8,128)S(1)} %get-tuple-element.23.p_in, f32[32,64,256]{2,1,0:T(8,128)S(1)} %get-tuple-element.24.vi_in, ...), custom_call_target="tpu_custom_call" | custom-call | tf_op jit(solution)/shard_map/advance/pallas_call | solution.py:651
  41.4 3.3 %finish.1 = (f32[32,64,256]{2,1,0:T(8,128)}, f32[32,64,256]{2,1,0:T(8,128)}, f32[32,64,256]{2,1,0:T(8,128)}, f32[32,64,256]{2,1,0:T(8,128)}) custom-call(f32[32,64,256]{2,1,0:T(8,128)S(1)} %get-tuple-element.36.p_in, f32[32,64,256]{2,1,0:T(8,128)S(1)} %get-tuple-element.37.vi, f32[32,64,256]{2,1,0:T(8,128)S(1)} %get-tuple-element.38.vx, ...), custom_call_target="tpu_custom_call" | custom-call | tf_op jit(solution)/shard_map/finish/pallas_call | solution.py:665

commit v3 on v1

--- a/solution.py
+++ b/solution.py
@@ -10,6 +10,7 @@
 LANES = 128
 SUBLANES = 8
 SLOT = 8
+NEAR = 8
 MESH = pl.DeviceIdType.MESH
 VMEM, HBM = pltpu.MemorySpace.VMEM, pltpu.MemorySpace.HBM
 F32 = jnp.float32
@@ -63,30 +64,33 @@
         velocity(p, v_in, v_out, buoyancy, planes - 1, tile, False)
 
 
-def velocity_edge(p, v_in, v_out, buoyancy, ahead_i, ahead_x):
+def velocity_next(p, v_in, v_out, buoyancy, ahead_i):
     planes, tiles = p.shape[0], p.shape[1] // SUBLANES
-    (vi, vx, _), (vi_out, vx_out, _) = v_in, v_out
-    i = planes - 1
     for tile in range(tiles):
         for h in range(2):
-            at = (i, rows(tile), cols(h))
-            rb = COURANT * buoyancy[at]
-            vi_out[at] = vi[at] - rb * (ahead_i[rows(tile), cols(h)] - p[at])
+            at = (planes - 1, rows(tile), cols(h))
+            v_out[0][at] = v_in[0][at] - COURANT * buoyancy[at] * (ahead_i[rows(tile), cols(h)] - p[at])
+
+
+def velocity_side(p, v_in, v_out, buoyancy, ahead_x, i):
     row = row_ids()
-
+    for h in range(2):
+        at = (i, rows(p.shape[1] // SUBLANES - 1), cols(h))
+        here = p[at]
+        ahead = jnp.where(
+            row < SUBLANES - 1,
+            pltpu.roll(here, SUBLANES - 1, 0),
+            jnp.broadcast_to(ahead_x[h, pl.ds(i, 1), :], here.shape),
+        )
+        v_out[1][at] = v_in[1][at] - COURANT * buoyancy[at] * (ahead - here)
+
+
+def between(planes, work, unroll):
     def plane(i, _):
-        for h in range(2):
-            at = (i, rows(tiles - 1), cols(h))
-            here = p[at]
-            ahead = jnp.where(
-                row < SUBLANES - 1,
-                pltpu.roll(here, SUBLANES - 1, 0),
-                jnp.broadcast_to(ahead_x[h, pl.ds(i, 1), :], here.shape),
-            )
-            vx_out[at] = vx[at] - COURANT * buoyancy[at] * (ahead - here)
+        work(i)
         return _
 
-    lax.fori_loop(0, planes, plane, 0, unroll=16)
+    lax.fori_loop(1, planes - 1, plane, 0, unroll=unroll)
 
 
 def ghosts(p, first_x, behind_i, behind_x, ghost_in, ghost_out, ghost_b):
@@ -128,26 +132,26 @@
     return strip
 
 
-def shell(planes, tiles, strip):
+def ends(planes, tiles, strip):
     for tile in range(tiles):
         strip(0, tile, True)
         strip(planes - 1, tile, False)
 
-    def plane(i, _):
+
+def sides(planes, tiles, strip):
+    def work(i):
         strip(i, 0, False)
         strip(i, tiles - 1, False)
-        return _
-
-    lax.fori_loop(1, planes - 1, plane, 0, unroll=15)
+
+    between(planes, work, 15)
 
 
 def core(planes, tiles, strip):
-    def plane(i, _):
+    def work(i):
         for tile in range(1, tiles - 1):
             strip(i, tile, False)
-        return _
-
-    lax.fori_loop(1, planes - 1, plane, 0, unroll=6)
+
+    between(planes, work, 6)
 
 
 def take_row(source, row, target):
@@ -274,7 +278,7 @@
     outbox, inbox, behind_i, ahead_i, behind_x, ahead_x, from_vi, from_bi, from_vx, from_bx,
     first_x, last_x, last_vx, last_bx,
     traces, owner, cell, resample,
-    load_sems, node_sems, send_sems, recv_sems, post_sem, mail_sem,
+    load_sems, node_sems, send_sems, recv_sems, post_sem, mail_sem, all_in,
 ):
     devices = lax.axis_size("xline") * lax.axis_size("inline")
     lines = lax.axis_size("inline")
@@ -294,40 +298,58 @@
     for load in node_loads + loads:
         load.start()
     barrier = pltpu.get_barrier_semaphore()
-    me = lax.axis_index("xline") * lines + lax.axis_index("inline")
-
-    def other(k):
-        there = lax.rem(me + k, devices)
-        return there, (there // lines, lax.rem(there, lines))
-
-    def greet(k, _):
-        pl.semaphore_signal(barrier, inc=1, device_id=other(k)[1], device_id_type=MESH)
-        return _
-
-    lax.fori_loop(1, devices, greet, 0)
+    xline, inline = lax.axis_index("xline"), lax.axis_index("inline")
+    wide, blocks = lax.axis_size("xline"), lines // NEAR
+    block, near = inline // NEAR, lax.rem(inline, NEAR)
+    me = xline * lines + inline
+    near_offsets = range(1, NEAR)
+    far_offsets = [(dx, dy) for dx in range(wide) for dy in range(blocks) if dx or dy]
+
+    def partner(dx, dy, dn):
+        return (lax.rem(xline + dx, wide), lax.rem(block + dy, blocks) * NEAR + lax.rem(near + dn, NEAR))
+
+    def greet(semaphore, offsets):
+        for offset in offsets:
+            pl.semaphore_signal(
+                semaphore, inc=1, device_id=partner(*offset), device_id_type=MESH
+            )
+
+    beside = [(0, 0, dn) for dn in near_offsets]
+    greet(barrier, beside + [(dx, dy, 0) for dx, dy in far_offsets])
 
     for load in node_loads:
         load.wait()
+    pl.semaphore_wait(barrier, len(beside) + len(far_offsets))
+    greet(all_in, beside)
     packed = pack(traces, owner, cell, resample, devices)
     for row in range(devices):
         outbox[row] = packed[row : row + 1]
     inbox[me] = outbox[me]
-
-    pl.semaphore_wait(barrier, devices - 1)
-
-    def post(k, _):
-        there, device = other(k)
+    pl.semaphore_wait(all_in, len(beside))
+
+    def hops(offset, length):
+        return min(offset, length - offset)
+
+    def post(dx, dy, dn):
+        device = partner(dx, dy, dn)
         pltpu.make_async_remote_copy(
-            src_ref=outbox.at[there],
+            src_ref=outbox.at[device[0] * lines + device[1]],
             dst_ref=inbox.at[me],
             send_sem=post_sem,
             recv_sem=mail_sem,
             device_id=device,
             device_id_type=MESH,
         ).start()
-        return _
-
-    lax.fori_loop(1, devices, post, 0)
+
+    for dx, dy in sorted(
+        [(0, 0)] + far_offsets, key=lambda o: -(hops(o[0], wide) + hops(o[1], blocks))
+    ):
+        def post_near(k, _):
+            post(dx, dy, lax.rem(k + 3, NEAR))
+            return _
+
+        own = int(dx == 0 and dy == 0)
+        lax.fori_loop(0, NEAR - own, post_near if not own else lambda k, _: (post(0, 0, k + 1), _)[1], 0)
 
     halo = Exchange(send_sems, recv_sems)
     for ref in (behind_i, from_vi, from_bi):
@@ -376,7 +398,10 @@
     lax.fori_loop(0, injected.shape[0] // 64, clear, 0)
 
     halo.finish()
-    velocity_edge(p, v, v, buoyancy, ahead_i, ahead_x)
+    velocity_next(p, v, v, buoyancy, ahead_i)
+    for i in (0, planes - 1):
+        velocity_side(p, v, v, buoyancy, ahead_x, i)
+    between(planes, lambda i: velocity_side(p, v, v, buoyancy, ahead_x, i), 15)
     ghosts(p, first_x, behind_i, behind_x, (from_vi, from_vx), (ghost_i, ghost_x), (from_bi, from_bx))
     ghost_bi[...] = from_bi[...]
     ghost_bx[...] = from_bx[...]
@@ -384,7 +409,8 @@
     def strip(i, tile, first):
         pressure(p, p, v, (ghost_i, ghost_x), modulus, i, tile, first, None)
 
-    shell(planes, tiles, strip)
+    ends(planes, tiles, strip)
+    sides(planes, tiles, strip)
     core(planes, tiles, strip)
 
     mail = pltpu.make_async_remote_copy(
@@ -392,7 +418,7 @@
         dst_ref=inbox.at[pl.ds(0, devices - 1)],
         send_sem=post_sem,
         recv_sem=mail_sem,
-        device_id=other(1)[1],
+        device_id=partner(0, 0, 1),
         device_id_type=MESH,
     )
     mail.wait_send()
@@ -463,10 +489,12 @@
     def _():
         ahead_x[...] = jnp.zeros_like(ahead_x)
 
-    def send(step):
+    def send_planes(step):
         halo.send_sems, halo.recv_sems = send_sems.at[step], recv_sems.at[step]
         halo.send(p.at[planes - 1], behind_i.at[step], 1, 1, 0)
         halo.send(p.at[0], ahead_i.at[step], 1, -1, 1)
+
+    def send_rows(step):
         take_row(p, 0, first_x.at[step])
         halo.send(first_x.at[step], ahead_x.at[step], 0, -1, 2)
         take_row(p, p.shape[1] - 1, last_x.at[step])
@@ -479,33 +507,46 @@
             at = (i, rows(tile), cols(h))
             p[at] = p_in[at] + COURANT * modulus[at] * spread(i, tile, h)
 
-    shell(planes, tiles, inject)
+    ends(planes, tiles, inject)
     halo.met(barrier)
-    send(0)
+    send_planes(0)
+    sides(planes, tiles, inject)
+    send_rows(0)
     core(planes, tiles, inject)
 
     v = (vi, vx, vd)
     for step in range(1, STEPS):
+        last = step == STEPS - 1
         v_in = (vi_in, vx_in, vd_in) if step == 1 else v
         ghost_in = (ghost_i_in, ghost_x_in) if step == 1 else (ghost_i, ghost_x)
+        spread = source(injected, p.shape[1], step)
+
+        def strip(i, tile, first):
+            pressure(p, p, v, (ghost_i, ghost_x), modulus, i, tile, first, spread)
+
         velocity_inside(p, v_in, v, buoyancy)
+        if last:
+            core(planes, tiles, strip)
         halo.finish()
-        velocity_edge(p, v_in, v, buoyancy, ahead_i.at[step - 1], ahead_x.at[step - 1])
+
+        def side(i):
+            velocity_side(p, v_in, v, buoyancy, ahead_x.at[step - 1], i)
+
+        velocity_next(p, v_in, v, buoyancy, ahead_i.at[step - 1])
+        side(0)
+        side(planes - 1)
         ghosts(
             p, first_x.at[step - 1], behind_i.at[step - 1], behind_x.at[step - 1],
             ghost_in, (ghost_i, ghost_x), (ghost_bi, ghost_bx),
         )
-
-        if step == STEPS - 1:
-            break
-        spread = source(injected, p.shape[1], step)
-
-        def strip(i, tile, first):
-            pressure(p, p, v, (ghost_i, ghost_x), modulus, i, tile, first, spread)
-
-        shell(planes, tiles, strip)
-        send(step)
-        core(planes, tiles, strip)
+        if not last:
+            ends(planes, tiles, strip)
+            send_planes(step)
+        between(planes, side, 15)
+        if not last:
+            sides(planes, tiles, strip)
+            send_rows(step)
+            core(planes, tiles, strip)
 
 
 def finish(
@@ -514,31 +555,29 @@
     p, sems,
 ):
     planes, tiles = p_in.shape[0], p_in.shape[1] // SUBLANES
-    copies = [
-        pltpu.make_async_copy(source, target, sems.at[k])
-        for k, (source, target) in enumerate(((vi, vi_out), (vx, vx_out), (vd, vd_out)))
-    ]
-    for copy in copies:
-        copy.start()
+    copies = []
+
+    def leave(source_ref, target):
+        copies.append(pltpu.make_async_copy(source_ref, target, sems.at[len(copies)]))
+        copies[-1].start()
+
+    for source_ref, target in ((vi, vi_out), (vx, vx_out), (vd, vd_out)):
+        leave(source_ref, target)
+    inner = pl.ds(1, planes - 2)
+    middle = (inner, pl.ds(SUBLANES, (tiles - 2) * SUBLANES))
+    leave(p_in.at[middle], p_out.at[middle])
     spread = source(injected, p_in.shape[1], STEPS - 1)
-    v, ghost = (vi, vx, vd), (ghost_i, ghost_x)
-    chunks = 4
-    size = planes // chunks
-
-    def plane(i, _):
-        for tile in range(tiles):
-            pressure(p_in, p, v, ghost, modulus, i, tile, False, spread)
-        return _
-
-    for chunk in range(chunks):
-        start = chunk * size
-        if chunk == 0:
-            for tile in range(tiles):
-                pressure(p_in, p, v, ghost, modulus, 0, tile, True, spread)
-        lax.fori_loop(max(start, 1), start + size, plane, 0, unroll=size if chunk else size - 1)
-        part = pl.ds(start, size)
-        copies.append(pltpu.make_async_copy(p.at[part], p_out.at[part], sems.at[3 + chunk]))
-        copies[-1].start()
+
+    def strip(i, tile, first):
+        pressure(p_in, p, (vi, vx, vd), (ghost_i, ghost_x), modulus, i, tile, first, spread)
+
+    ends(planes, tiles, strip)
+    for end in (0, planes - 1):
+        leave(p.at[end], p_out.at[end])
+    sides(planes, tiles, strip)
+    for tile in (0, tiles - 1):
+        side = (inner, rows(tile))
+        leave(p.at[side], p_out.at[side])
     for copy in copies:
         copy.wait()
 
@@ -572,7 +611,7 @@
             VMEM(traces.shape, F32), VMEM((1, held), jnp.int32), VMEM((1, held), jnp.int32),
             VMEM(resample.shape, F32),
         ]
-        + [dma((6,)), dma((4,)), dma((8,)), dma((8,)), dma, dma],
+        + [dma((6,)), dma((4,)), dma((8,)), dma((8,)), dma, dma, pltpu.SemaphoreType.REGULAR],
         compiler_params=pltpu.CompilerParams(collective_id=0, has_side_effects=True, vmem_limit_bytes=LIMIT),
         name="route",
     )(
@@ -615,7 +654,7 @@
         out_shape=[HBM(field, F32)] * 4,
         in_specs=[vmem] * 8,
         out_specs=[hbm] * 4,
-        scratch_shapes=[VMEM(field, F32), dma((7,))],
+        scratch_shapes=[VMEM(field, F32), dma((8,))],
         compiler_params=pltpu.CompilerParams(vmem_limit_bytes=LIMIT),
         name="finish",
     )(*fields, ghost_i, ghost_x, modulus, injected)

time: 45.2 us -> 44.1 us (0.976)
  Pallas kernels: 44.4 us -> 43.3 us
    pallas_call x1, Pallas kernels: 15.2 us -> 14.3 us  [shards(): pl.pallas_call(advance, out_shape=[VMEM(field, F32)] * 4 + [VMEM(plane, F...]
where the time goes in v3:
time: 44.1 us; the launch traced here: 44 us
  Pallas kernels  43.3 us (98%)
  between operations  0.66 us (1%)
    pallas_call x1, Pallas kernels, shards(): pl.pallas_call(route, out_shape=[VMEM(field, F32)] * 6 + [VMEM(plane, F32...  18.2 us
    pallas_call x1, Pallas kernels, shards(): pl.pallas_call(advance, out_shape=[VMEM(field, F32)] * 4 + [VMEM(plane, F...  14.3 us
    pallas_call x1, Pallas kernels, shards(): pl.pallas_call(scatter, out_shape=VMEM(injection, F32), in_specs=[vmem] *...  7.54 us
    pallas_call x1, Pallas kernels, shards(): pl.pallas_call(finish, out_shape=[HBM(field, F32)] * 4, in_specs=[vmem] *...  3.33 us

profile of v3, /device:TPU:8, one launch (start us, length us, event | category | flops | bytes accessed | tf_op | source)
XLA Modules:
  0.0 44.0 jit_solution(5816530875110712070)
XLA Ops:
  0.6 18.2 %route.1 = (f32[32,64,256]{2,1,0:T(8,128)S(1)}, f32[32,64,256]{2,1,0:T(8,128)S(1)}, f32[32,64,256]{2,1,0:T(8,128)S(1)}, f32[32,64,256]{2,1,0:T(8,128)S(1)}, f32[...) custom-call(f32[32,64,256]{2,1,0:T(8,128)} %p_hbm.1, ...), custom_call_target="tpu_custom_call" | custom-call | tf_op jit(solution)/shard_map/route/pallas_call | solution.py:598
  18.8 7.5 %scatter.1.injected = f32[16384,128]{1,0:T(8,128)S(1)} custom-call(s32[16,128]{1,0:T(8,128)S(1)} %get-tuple-element.33.index_ref, f32[128,128]{1,0:T(8,128)S(1)} %get-tuple-element.34.values, f32[16384,128]{1,0:T(8,128)S(1)} %get-tuple-element.35._), custom_call_target="tpu_custom_call", output_to_operand_aliasing={{}: (2, {})} | custom-call | tf_op jit(solution)/shard_map/scatter/pallas_call | solution.py:627
  26.4 14.3 %advance.1 = (f32[32,64,256]{2,1,0:T(8,128)S(1)}, f32[32,64,256]{2,1,0:T(8,128)S(1)}, f32[32,64,256]{2,1,0:T(8,128)S(1)}, f32[32,64,256]{2,1,0:T(8,128)S(1)}, f3...) custom-call(f32[32,64,256]{2,1,0:T(8,128)S(1)} %get-tuple-element.23.p_in, f32[32,64,256]{2,1,0:T(8,128)S(1)} %get-tuple-element.24.vi_in, ...), custom_call_target="tpu_custom_call" | custom-call | tf_op jit(solution)/shard_map/advance/pallas_call | solution.py:638
  40.7 3.3 %finish.1 = (f32[32,64,256]{2,1,0:T(8,128)}, f32[32,64,256]{2,1,0:T(8,128)}, f32[32,64,256]{2,1,0:T(8,128)}, f32[32,64,256]{2,1,0:T(8,128)}) custom-call(f32[32,64,256]{2,1,0:T(8,128)S(1)} %get-tuple-element.36.p_in, f32[32,64,256]{2,1,0:T(8,128)S(1)} %get-tuple-element.37.vi, f32[32,64,256]{2,1,0:T(8,128)S(1)} %get-tuple-element.38.vx, ...), custom_call_target="tpu_custom_call" | custom-call | tf_op jit(solution)/shard_map/finish/pallas_call | solution.py:652

commit v4 on v3

--- a/solution.py
+++ b/solution.py
@@ -14,7 +14,7 @@
 MESH = pl.DeviceIdType.MESH
 VMEM, HBM = pltpu.MemorySpace.VMEM, pltpu.MemorySpace.HBM
 F32 = jnp.float32
-LIMIT = 16 * 2**20
+MIB = 2**20
 
 
 def lane_ids():
@@ -127,7 +127,8 @@
 def source(injected, wide, step):
     def strip(i, tile, h):
         row = ((i * wide + tile * SUBLANES) * 2 + h) * STEPS + step
-        return injected[pl.ds(row, SUBLANES, stride=2 * STEPS), :]
+        at = pl.ds(row, SUBLANES, stride=2 * STEPS)
+        return injected[0][at, :] + injected[1][at, :]
 
     return strip
 
@@ -274,7 +275,7 @@
 
 def route(
     p_hbm, vi_hbm, vx_hbm, vd_hbm, m_hbm, b_hbm, traces_hbm, owner_hbm, cell_hbm, resample_hbm,
-    p, vi, vx, vd, modulus, buoyancy, ghost_i, ghost_x, ghost_bi, ghost_bx, index, values, injected,
+    p, vi, vx, vd, modulus, buoyancy, ghost_i, ghost_x, ghost_bi, ghost_bx, index, values, injected_a, injected_b,
     outbox, inbox, behind_i, ahead_i, behind_x, ahead_x, from_vi, from_bi, from_vx, from_bx,
     first_x, last_x, last_vx, last_bx,
     traces, owner, cell, resample,
@@ -283,10 +284,11 @@
     devices = lax.axis_size("xline") * lax.axis_size("inline")
     lines = lax.axis_size("inline")
     planes, tiles = p.shape[0], p.shape[1] // SUBLANES
+    injected = (injected_a, injected_b)
     loads = [
         pltpu.make_async_copy(source, target, load_sems.at[k])
         for k, (source, target) in enumerate(
-            ((p_hbm, p), (b_hbm, buoyancy), (vi_hbm, vi), (vx_hbm, vx), (vd_hbm, vd), (m_hbm, modulus))
+            ((p_hbm, p), (b_hbm, buoyancy), (vx_hbm, vx), (vi_hbm, vi), (vd_hbm, vd), (m_hbm, modulus))
         )
     ]
     node_loads = [
@@ -295,7 +297,7 @@
             ((owner_hbm, owner), (cell_hbm, cell.at[0]), (resample_hbm, resample), (traces_hbm, traces))
         )
     ]
-    for load in node_loads + loads:
+    for load in node_loads:
         load.start()
     barrier = pltpu.get_barrier_semaphore()
     xline, inline = lax.axis_index("xline"), lax.axis_index("inline")
@@ -317,8 +319,12 @@
     beside = [(0, 0, dn) for dn in near_offsets]
     greet(barrier, beside + [(dx, dy, 0) for dx, dy in far_offsets])
 
+    for load in loads[:2]:
+        load.start()
     for load in node_loads:
         load.wait()
+    for load in loads[2:]:
+        load.start()
     pl.semaphore_wait(barrier, len(beside) + len(far_offsets))
     greet(all_in, beside)
     packed = pack(traces, owner, cell, resample, devices)
@@ -326,6 +332,30 @@
         outbox[row] = packed[row : row + 1]
     inbox[me] = outbox[me]
     pl.semaphore_wait(all_in, len(beside))
+
+    halo = Exchange(send_sems, recv_sems)
+    for ref in (behind_i, from_vi, from_bi):
+        @pl.when(jnp.logical_not(halo.has(1, -1)))
+        def _():
+            ref[...] = jnp.zeros_like(ref)
+    for ref in (behind_x, from_vx, from_bx):
+        @pl.when(jnp.logical_not(halo.has(0, -1)))
+        def _():
+            ref[...] = jnp.zeros_like(ref)
+
+    @pl.when(jnp.logical_not(halo.has(1, 1)))
+    def _():
+        ahead_i[...] = jnp.zeros_like(ahead_i)
+
+    @pl.when(jnp.logical_not(halo.has(0, 1)))
+    def _():
+        ahead_x[...] = jnp.zeros_like(ahead_x)
+
+    last = planes - 1
+    halo.send(p_hbm.at[last], behind_i, 1, 1, 0)
+    halo.send(p_hbm.at[0], ahead_i, 1, -1, 1)
+    halo.send(vi_hbm.at[last], from_vi, 1, 1, 6)
+    halo.send(b_hbm.at[last], from_bi, 1, 1, 4)
 
     def hops(offset, length):
         return min(offset, length - offset)
@@ -351,52 +381,34 @@
         own = int(dx == 0 and dy == 0)
         lax.fori_loop(0, NEAR - own, post_near if not own else lambda k, _: (post(0, 0, k + 1), _)[1], 0)
 
-    halo = Exchange(send_sems, recv_sems)
-    for ref in (behind_i, from_vi, from_bi):
-        @pl.when(jnp.logical_not(halo.has(1, -1)))
-        def _():
-            ref[...] = jnp.zeros_like(ref)
-    for ref in (behind_x, from_vx, from_bx):
-        @pl.when(jnp.logical_not(halo.has(0, -1)))
-        def _():
-            ref[...] = jnp.zeros_like(ref)
-
-    @pl.when(jnp.logical_not(halo.has(1, 1)))
-    def _():
-        ahead_i[...] = jnp.zeros_like(ahead_i)
-
-    @pl.when(jnp.logical_not(halo.has(0, 1)))
-    def _():
-        ahead_x[...] = jnp.zeros_like(ahead_x)
-
     loads[0].wait()
-    halo.send(p.at[planes - 1], behind_i, 1, 1, 0)
-    halo.send(p.at[0], ahead_i, 1, -1, 1)
     take_row(p, 0, first_x)
     halo.send(first_x, ahead_x, 0, -1, 2)
     take_row(p, p.shape[1] - 1, last_x)
     halo.send(last_x, behind_x, 0, 1, 3)
     loads[1].wait()
-    halo.send(buoyancy.at[planes - 1], from_bi, 1, 1, 4)
     take_row(buoyancy, p.shape[1] - 1, last_bx)
     halo.send(last_bx, from_bx, 0, 1, 5)
     loads[2].wait()
-    halo.send(vi.at[planes - 1], from_vi, 1, 1, 6)
-    loads[3].wait()
     take_row(vx, p.shape[1] - 1, last_vx)
     halo.send(last_vx, from_vx, 0, 1, 7)
+
+    def clear(k, _):
+        for ref in injected:
+            ref[pl.ds(pl.multiple_of(k * 64, 64), 64), :] = jnp.zeros((64, LANES), F32)
+        return _
+
+    lax.fori_loop(0, injected[0].shape[0] // 64, clear, 0)
+    loads[3].wait()
     loads[4].wait()
-    loads[5].wait()
-
     v = (vi, vx, vd)
     velocity_inside(p, v, v, buoyancy)
-
-    def clear(k, _):
-        injected[pl.ds(pl.multiple_of(k * 64, 64), 64), :] = jnp.zeros((64, LANES), F32)
-        return _
-
-    lax.fori_loop(0, injected.shape[0] // 64, clear, 0)
-
+    loads[5].wait()
+
+    def strip(i, tile, first):
+        pressure(p, p, v, (ghost_i, ghost_x), modulus, i, tile, first, None)
+
+    core(planes, tiles, strip)
     halo.finish()
     velocity_next(p, v, v, buoyancy, ahead_i)
     for i in (0, planes - 1):
@@ -405,13 +417,8 @@
     ghosts(p, first_x, behind_i, behind_x, (from_vi, from_vx), (ghost_i, ghost_x), (from_bi, from_bx))
     ghost_bi[...] = from_bi[...]
     ghost_bx[...] = from_bx[...]
-
-    def strip(i, tile, first):
-        pressure(p, p, v, (ghost_i, ghost_x), modulus, i, tile, first, None)
-
     ends(planes, tiles, strip)
     sides(planes, tiles, strip)
-    core(planes, tiles, strip)
 
     mail = pltpu.make_async_remote_copy(
         src_ref=outbox.at[pl.ds(0, devices - 1)],
@@ -427,12 +434,13 @@
     index[...] = values[pl.ds(STEPS, LANES // SLOT, stride=SLOT), :].astype(jnp.int32)
 
 
-def scatter(index_ref, values, _, injected, index, sem):
+def scatter(index_ref, values, _a, _b, injected_a, injected_b, index, sem):
     load = pltpu.make_async_copy(index_ref, index, sem)
     load.start()
-    devices = values.shape[1]
+    injected = (injected_a, injected_b)
+    share = values.shape[1] // len(injected)
     lane = lax.broadcasted_iota(jnp.int32, (STEPS, LANES), 1)
-    slots, group = 15, 3
+    slots, group = 15, 2
 
     def spread(d):
         pick = jnp.full((SUBLANES, LANES), d, jnp.int32)
@@ -441,34 +449,41 @@
             for q in range(slots)
         ]
 
+    def add(target, d, now, numbers):
+        tiles, adds = [], []
+        for q in numbers:
+            cell = index[q, d]
+            tiles.append(lax.shift_right_logical(cell, 7))
+            adds.append(jnp.where(lane == (cell & (LANES - 1)), now[q], 0.0))
+        spots = [pl.ds(pl.multiple_of(tile * STEPS, STEPS), STEPS) for tile in tiles]
+        old = [target[spot, :] for spot in spots]
+        for b in range(len(numbers)):
+            new = old[b] + adds[b]
+            for a in range(b):
+                new = new + jnp.where(tiles[a] == tiles[b], adds[a], 0.0)
+            target[spots[b], :] = new
+
     def sender(d, now):
-        later = spread(jnp.minimum(d + 1, devices - 1))
+        later = [
+            spread(jnp.minimum(d + 1, share - 1) + k * share) for k in range(len(injected))
+        ]
         for start in range(0, slots, group):
-            tiles, adds = [], []
-            for q in range(start, start + group):
-                cell = index[q, d]
-                tiles.append(lax.shift_right_logical(cell, 7))
-                adds.append(jnp.where(lane == (cell & (LANES - 1)), now[q], 0.0))
-            spots = [pl.ds(pl.multiple_of(tile * STEPS, STEPS), STEPS) for tile in tiles]
-            old = [injected[spot, :] for spot in spots]
-            for b in range(group):
-                new = old[b] + adds[b]
-                for a in range(b):
-                    new = new + jnp.where(tiles[a] == tiles[b], adds[a], 0.0)
-                injected[spots[b], :] = new
+            for k, target in enumerate(injected):
+                add(target, d + k * share, now[k], range(start, min(start + group, slots)))
         return later
 
-    first = spread(0)
+    first = [spread(k * share) for k in range(len(injected))]
     load.wait()
-    lax.fori_loop(0, devices, sender, first, unroll=4)
+    lax.fori_loop(0, share, sender, first, unroll=4)
 
 
 def advance(
-    p_in, vi_in, vx_in, vd_in, modulus, buoyancy, ghost_i_in, ghost_x_in, ghost_bi, ghost_bx, injected,
+    p_in, vi_in, vx_in, vd_in, modulus, buoyancy, ghost_i_in, ghost_x_in, ghost_bi, ghost_bx, injected_a, injected_b,
     p, vi, vx, vd, ghost_i, ghost_x,
     behind_i, ahead_i, behind_x, ahead_x, first_x, last_x, send_sems, recv_sems,
 ):
     planes, tiles = p.shape[0], p.shape[1] // SUBLANES
+    injected = (injected_a, injected_b)
     halo = Exchange(None, None)
     barrier = pltpu.get_barrier_semaphore()
     halo.greet(barrier)
@@ -550,7 +565,7 @@
 
 
 def finish(
-    p_in, vi, vx, vd, ghost_i, ghost_x, modulus, injected,
+    p_in, vi, vx, vd, ghost_i, ghost_x, modulus, injected_a, injected_b,
     p_out, vi_out, vx_out, vd_out,
     p, sems,
 ):
@@ -566,7 +581,7 @@
     inner = pl.ds(1, planes - 2)
     middle = (inner, pl.ds(SUBLANES, (tiles - 2) * SUBLANES))
     leave(p_in.at[middle], p_out.at[middle])
-    spread = source(injected, p_in.shape[1], STEPS - 1)
+    spread = source((injected_a, injected_b), p_in.shape[1], STEPS - 1)
 
     def strip(i, tile, first):
         pressure(p_in, p, (vi, vx, vd), (ghost_i, ghost_x), modulus, i, tile, first, spread)
@@ -599,9 +614,10 @@
         route,
         out_shape=[VMEM(field, F32)] * 6
         + [VMEM(plane, F32), VMEM(column, F32)] * 2
-        + [VMEM((LANES // SLOT, devices), jnp.int32), VMEM((LANES, devices), F32), VMEM(injection, F32)],
+        + [VMEM((LANES // SLOT, devices), jnp.int32), VMEM((LANES, devices), F32)]
+        + [VMEM(injection, F32)] * 2,
         in_specs=[hbm] * 10,
-        out_specs=[vmem] * 13,
+        out_specs=[vmem] * 14,
         scratch_shapes=[VMEM((devices, 1, LANES), F32)] * 2
         + [VMEM(plane, F32)] * 2
         + [VMEM(column, F32)] * 2
@@ -612,7 +628,7 @@
             VMEM(resample.shape, F32),
         ]
         + [dma((6,)), dma((4,)), dma((8,)), dma((8,)), dma, dma, pltpu.SemaphoreType.REGULAR],
-        compiler_params=pltpu.CompilerParams(collective_id=0, has_side_effects=True, vmem_limit_bytes=LIMIT),
+        compiler_params=pltpu.CompilerParams(collective_id=0, has_side_effects=True, vmem_limit_bytes=8 * MIB),
         name="route",
     )(
         *(
@@ -623,41 +639,41 @@
             )
         )
     )
-    *fields, index, values, cleared = state
+    *fields, index, values, cleared_a, cleared_b = state
     injected = pl.pallas_call(
         scatter,
-        out_shape=VMEM(injection, F32),
-        in_specs=[vmem] * 3,
-        out_specs=vmem,
+        out_shape=[VMEM(injection, F32)] * 2,
+        in_specs=[vmem] * 4,
+        out_specs=[vmem] * 2,
         scratch_shapes=[pltpu.SMEM((LANES // SLOT, devices), jnp.int32), dma],
-        input_output_aliases={2: 0},
-        compiler_params=pltpu.CompilerParams(vmem_limit_bytes=LIMIT),
+        input_output_aliases={2: 0, 3: 1},
+        compiler_params=pltpu.CompilerParams(vmem_limit_bytes=2 * MIB),
         name="scatter",
-    )(index, values, cleared)
+    )(index, values, cleared_a, cleared_b)
     rounds = STEPS - 1
     *fields, ghost_i, ghost_x = pl.pallas_call(
         advance,
         out_shape=[VMEM(field, F32)] * 4 + [VMEM(plane, F32), VMEM(column, F32)],
-        in_specs=[vmem] * 11,
+        in_specs=[vmem] * 12,
         out_specs=[vmem] * 6,
         scratch_shapes=[VMEM((rounds, *plane), F32)] * 2
         + [VMEM((rounds, *column), F32)] * 4
         + [dma((rounds, 4)), dma((rounds, 4))],
         compiler_params=pltpu.CompilerParams(
-            collective_id=1, has_side_effects=True, vmem_limit_bytes=LIMIT
+            collective_id=1, has_side_effects=True, vmem_limit_bytes=4 * MIB
         ),
         name="advance",
-    )(*fields, injected)
+    )(*fields, *injected)
     modulus = state[4]
     return pl.pallas_call(
         finish,
         out_shape=[HBM(field, F32)] * 4,
-        in_specs=[vmem] * 8,
+        in_specs=[vmem] * 9,
         out_specs=[hbm] * 4,
         scratch_shapes=[VMEM(field, F32), dma((8,))],
-        compiler_params=pltpu.CompilerParams(vmem_limit_bytes=LIMIT),
+        compiler_params=pltpu.CompilerParams(vmem_limit_bytes=4 * MIB),
         name="finish",
-    )(*fields, ghost_i, ghost_x, modulus, injected)
+    )(*fields, ghost_i, ghost_x, modulus, *injected)
 
 
 def solution(mesh):

time: 44.1 us -> 41.7 us (0.946)
  Pallas kernels: 43.3 us -> 40.9 us
    pallas_call x1, Pallas kernels: 18.2 us -> 16.9 us  [shards(): pl.pallas_call(route, out_shape=[VMEM(field, F32)] * 6 + [VMEM(plane, F32...]
    pallas_call x1, Pallas kernels: 7.54 us -> 6.36 us  [shards(): pl.pallas_call(scatter, out_shape=[VMEM(injection, F32)] * 2, in_specs=[v...]
where the time goes in v4:
time: 41.7 us; the launch traced here: 41.6 us
  Pallas kernels  40.9 us (98%)
  between operations  0.66 us (2%)
    pallas_call x1, Pallas kernels, shards(): pl.pallas_call(route, out_shape=[VMEM(field, F32)] * 6 + [VMEM(plane, F32...  16.9 us
    pallas_call x1, Pallas kernels, shards(): pl.pallas_call(advance, out_shape=[VMEM(field, F32)] * 4 + [VMEM(plane, F...  14.3 us
    pallas_call x1, Pallas kernels, shards(): pl.pallas_call(scatter, out_shape=[VMEM(injection, F32)] * 2, in_specs=[v...  6.36 us
    pallas_call x1, Pallas kernels, shards(): pl.pallas_call(finish, out_shape=[HBM(field, F32)] * 4, in_specs=[vmem] *...  3.33 us

profile of v4, /device:TPU:8, one launch (start us, length us, event | category | flops | bytes accessed | tf_op | source)
XLA Modules:
  0.0 41.6 jit_solution(12986677982776152897)
XLA Ops:
  0.6 16.9 %route.1 = (f32[32,64,256]{2,1,0:T(8,128)S(1)}, f32[32,64,256]{2,1,0:T(8,128)S(1)}, f32[32,64,256]{2,1,0:T(8,128)S(1)}, f32[32,64,256]{2,1,0:T(8,128)S(1)}, f32[...) custom-call(f32[32,64,256]{2,1,0:T(8,128)} %p_hbm.1, ...), custom_call_target="tpu_custom_call" | custom-call | tf_op jit(solution)/shard_map/route/pallas_call | solution.py:613
  17.6 6.4 %scatter.1 = (f32[16384,128]{1,0:T(8,128)S(1)}, f32[16384,128]{1,0:T(8,128)S(1)}) custom-call(s32[16,128]{1,0:T(8,128)S(1)} %get-tuple-element.36.index_ref, f32[128,128]{1,0:T(8,128)S(1)} %get-tuple-element.37.values, f32[16384,128]{1,0:T(8,128)S(1)} %get-tuple-element.38._a, ...), custom_call_target="tpu_custom_call", output_to_operand_aliasing={{0}: (2, {}), {1}: (3, {})} | custom-call | tf_op jit(solution)/shard_map/scatter/pallas_call | solution.py:643
  23.9 14.3 %advance.1 = (f32[32,64,256]{2,1,0:T(8,128)S(1)}, f32[32,64,256]{2,1,0:T(8,128)S(1)}, f32[32,64,256]{2,1,0:T(8,128)S(1)}, f32[32,64,256]{2,1,0:T(8,128)S(1)}, f3...) custom-call(f32[32,64,256]{2,1,0:T(8,128)S(1)} %get-tuple-element.26.p_in, f32[32,64,256]{2,1,0:T(8,128)S(1)} %get-tuple-element.27.vi_in, ...), custom_call_target="tpu_custom_call" | custom-call | tf_op jit(solution)/shard_map/advance/pallas_call | solution.py:654
  38.2 3.3 %finish.1 = (f32[32,64,256]{2,1,0:T(8,128)}, f32[32,64,256]{2,1,0:T(8,128)}, f32[32,64,256]{2,1,0:T(8,128)}, f32[32,64,256]{2,1,0:T(8,128)}) custom-call(f32[32,64,256]{2,1,0:T(8,128)S(1)} %get-tuple-element.42.p_in, f32[32,64,256]{2,1,0:T(8,128)S(1)} %get-tuple-element.43.vi, f32[32,64,256]{2,1,0:T(8,128)S(1)} %get-tuple-element.44.vx, ...), custom_call_target="tpu_custom_call" | custom-call | tf_op jit(solution)/shard_map/finish/pallas_call | solution.py:668

commit v5 on v4

--- a/solution.py
+++ b/solution.py
@@ -144,7 +144,7 @@
         strip(i, 0, False)
         strip(i, tiles - 1, False)
 
-    between(planes, work, 15)
+    between(planes, work, planes - 2)
 
 
 def core(planes, tiles, strip):
@@ -454,7 +454,8 @@
         for q in numbers:
             cell = index[q, d]
             tiles.append(lax.shift_right_logical(cell, 7))
-            adds.append(jnp.where(lane == (cell & (LANES - 1)), now[q], 0.0))
+            depth = jnp.full(lane.shape, cell, jnp.int32) & (LANES - 1)
+            adds.append(jnp.where(lane == depth, now[q], 0.0))
         spots = [pl.ds(pl.multiple_of(tile * STEPS, STEPS), STEPS) for tile in tiles]
         old = [target[spot, :] for spot in spots]
         for b in range(len(numbers)):
@@ -523,9 +524,9 @@
             p[at] = p_in[at] + COURANT * modulus[at] * spread(i, tile, h)
 
     ends(planes, tiles, inject)
+    sides(planes, tiles, inject)
     halo.met(barrier)
     send_planes(0)
-    sides(planes, tiles, inject)
     send_rows(0)
     core(planes, tiles, inject)
 
@@ -540,8 +541,6 @@
             pressure(p, p, v, (ghost_i, ghost_x), modulus, i, tile, first, spread)
 
         velocity_inside(p, v_in, v, buoyancy)
-        if last:
-            core(planes, tiles, strip)
         halo.finish()
 
         def side(i):
@@ -557,7 +556,7 @@
         if not last:
             ends(planes, tiles, strip)
             send_planes(step)
-        between(planes, side, 15)
+        between(planes, side, planes - 2)
         if not last:
             sides(planes, tiles, strip)
             send_rows(step)
@@ -578,21 +577,23 @@
 
     for source_ref, target in ((vi, vi_out), (vx, vx_out), (vd, vd_out)):
         leave(source_ref, target)
-    inner = pl.ds(1, planes - 2)
-    middle = (inner, pl.ds(SUBLANES, (tiles - 2) * SUBLANES))
-    leave(p_in.at[middle], p_out.at[middle])
     spread = source((injected_a, injected_b), p_in.shape[1], STEPS - 1)
-
-    def strip(i, tile, first):
-        pressure(p_in, p, (vi, vx, vd), (ghost_i, ghost_x), modulus, i, tile, first, spread)
-
-    ends(planes, tiles, strip)
-    for end in (0, planes - 1):
-        leave(p.at[end], p_out.at[end])
-    sides(planes, tiles, strip)
-    for tile in (0, tiles - 1):
-        side = (inner, rows(tile))
-        leave(p.at[side], p_out.at[side])
+    size = planes // 4
+
+    def plane(i, first):
+        for tile in range(tiles):
+            pressure(p_in, p, (vi, vx, vd), (ghost_i, ghost_x), modulus, i, tile, first, spread)
+
+    def inner(i, _):
+        plane(i, False)
+        return _
+
+    for start in range(0, planes, size):
+        if start == 0:
+            plane(0, True)
+        head = max(start, 1)
+        lax.fori_loop(head, start + size, inner, 0, unroll=start + size - head)
+        leave(p.at[pl.ds(start, size)], p_out.at[pl.ds(start, size)])
     for copy in copies:
         copy.wait()
 

time: 41.7 us -> 41 us (0.983)
  Pallas kernels: 40.9 us -> 40.3 us
    pallas_call x1, Pallas kernels: 6.36 us -> 5.8 us  [shards(): pl.pallas_call(scatter, out_shape=[VMEM(injection, F32)] * 2, in_specs=[v...]
where the time goes in v5:
time: 41 us; the launch traced here: 40.9 us
  Pallas kernels  40.3 us (98%)
  between operations  0.66 us (2%)
    pallas_call x1, Pallas kernels, shards(): pl.pallas_call(route, out_shape=[VMEM(field, F32)] * 6 + [VMEM(plane, F32...  16.8 us
    pallas_call x1, Pallas kernels, shards(): pl.pallas_call(advance, out_shape=[VMEM(field, F32)] * 4 + [VMEM(plane, F...  14.3 us
    pallas_call x1, Pallas kernels, shards(): pl.pallas_call(scatter, out_shape=[VMEM(injection, F32)] * 2, in_specs=[v...  5.8 us
    pallas_call x1, Pallas kernels, shards(): pl.pallas_call(finish, out_shape=[HBM(field, F32)] * 4, in_specs=[vmem] *...  3.35 us

profile of v5, /device:TPU:8, one launch (start us, length us, event | category | flops | bytes accessed | tf_op | source)
XLA Modules:
  0.0 40.9 jit_solution(15425838174791365158)
XLA Ops:
  0.6 16.8 %route.1 = (f32[32,64,256]{2,1,0:T(8,128)S(1)}, f32[32,64,256]{2,1,0:T(8,128)S(1)}, f32[32,64,256]{2,1,0:T(8,128)S(1)}, f32[32,64,256]{2,1,0:T(8,128)S(1)}, f32[...) custom-call(f32[32,64,256]{2,1,0:T(8,128)} %p_hbm.1, ...), custom_call_target="tpu_custom_call" | custom-call | tf_op jit(solution)/shard_map/route/pallas_call | solution.py:614
  17.5 5.8 %scatter.1 = (f32[16384,128]{1,0:T(8,128)S(1)}, f32[16384,128]{1,0:T(8,128)S(1)}) custom-call(s32[16,128]{1,0:T(8,128)S(1)} %get-tuple-element.36.index_ref, f32[128,128]{1,0:T(8,128)S(1)} %get-tuple-element.37.values, f32[16384,128]{1,0:T(8,128)S(1)} %get-tuple-element.38._a, ...), custom_call_target="tpu_custom_call", output_to_operand_aliasing={{0}: (2, {}), {1}: (3, {})} | custom-call | tf_op jit(solution)/shard_map/scatter/pallas_call | solution.py:644
  23.3 14.3 %advance.1 = (f32[32,64,256]{2,1,0:T(8,128)S(1)}, f32[32,64,256]{2,1,0:T(8,128)S(1)}, f32[32,64,256]{2,1,0:T(8,128)S(1)}, f32[32,64,256]{2,1,0:T(8,128)S(1)}, f3...) custom-call(f32[32,64,256]{2,1,0:T(8,128)S(1)} %get-tuple-element.26.p_in, f32[32,64,256]{2,1,0:T(8,128)S(1)} %get-tuple-element.27.vi_in, ...), custom_call_target="tpu_custom_call" | custom-call | tf_op jit(solution)/shard_map/advance/pallas_call | solution.py:655
  37.6 3.4 %finish.1 = (f32[32,64,256]{2,1,0:T(8,128)}, f32[32,64,256]{2,1,0:T(8,128)}, f32[32,64,256]{2,1,0:T(8,128)}, f32[32,64,256]{2,1,0:T(8,128)}) custom-call(f32[32,64,256]{2,1,0:T(8,128)S(1)} %get-tuple-element.42.p_in, f32[32,64,256]{2,1,0:T(8,128)S(1)} %get-tuple-element.43.vi, f32[32,64,256]{2,1,0:T(8,128)S(1)} %get-tuple-element.44.vx, ...), custom_call_target="tpu_custom_call" | custom-call | tf_op jit(solution)/shard_map/finish/pallas_call | solution.py:669

commit v6 on v5

--- a/solution.py
+++ b/solution.py
@@ -279,7 +279,7 @@
     outbox, inbox, behind_i, ahead_i, behind_x, ahead_x, from_vi, from_bi, from_vx, from_bx,
     first_x, last_x, last_vx, last_bx,
     traces, owner, cell, resample,
-    load_sems, node_sems, send_sems, recv_sems, post_sem, mail_sem, all_in,
+    load_sems, node_sems, send_sems, recv_sems, post_sem, mail_sem,
 ):
     devices = lax.axis_size("xline") * lax.axis_size("inline")
     lines = lax.axis_size("inline")
@@ -304,34 +304,35 @@
     wide, blocks = lax.axis_size("xline"), lines // NEAR
     block, near = inline // NEAR, lax.rem(inline, NEAR)
     me = xline * lines + inline
-    near_offsets = range(1, NEAR)
-    far_offsets = [(dx, dy) for dx in range(wide) for dy in range(blocks) if dx or dy]
+    xlines = [lax.rem(xline + k, wide) for k in range(wide)]
+    block_starts = [lax.rem(block + k, blocks) * NEAR for k in range(blocks)]
+    nears = [lax.rem(near + k, NEAR) for k in range(NEAR)]
+
+    def hops(offset, length):
+        return min(offset, length - offset)
+
+    offsets = [(dx, dy, dn) for dx in range(wide) for dy in range(blocks) for dn in range(NEAR)]
+    offsets = sorted(
+        offsets[1:],
+        key=lambda o: -(hops(o[0], wide) + hops(o[1], blocks) + hops(o[2], NEAR) / 2),
+    )
 
     def partner(dx, dy, dn):
-        return (lax.rem(xline + dx, wide), lax.rem(block + dy, blocks) * NEAR + lax.rem(near + dn, NEAR))
-
-    def greet(semaphore, offsets):
-        for offset in offsets:
-            pl.semaphore_signal(
-                semaphore, inc=1, device_id=partner(*offset), device_id_type=MESH
-            )
-
-    beside = [(0, 0, dn) for dn in near_offsets]
-    greet(barrier, beside + [(dx, dy, 0) for dx, dy in far_offsets])
-
+        return (xlines[dx], block_starts[dy] + nears[dn])
+
+    for offset in offsets:
+        pl.semaphore_signal(barrier, inc=1, device_id=partner(*offset), device_id_type=MESH)
     for load in loads[:2]:
         load.start()
     for load in node_loads:
         load.wait()
     for load in loads[2:]:
         load.start()
-    pl.semaphore_wait(barrier, len(beside) + len(far_offsets))
-    greet(all_in, beside)
     packed = pack(traces, owner, cell, resample, devices)
     for row in range(devices):
         outbox[row] = packed[row : row + 1]
     inbox[me] = outbox[me]
-    pl.semaphore_wait(all_in, len(beside))
+    pl.semaphore_wait(barrier, len(offsets))
 
     halo = Exchange(send_sems, recv_sems)
     for ref in (behind_i, from_vi, from_bi):
@@ -356,9 +357,6 @@
     halo.send(p_hbm.at[0], ahead_i, 1, -1, 1)
     halo.send(vi_hbm.at[last], from_vi, 1, 1, 6)
     halo.send(b_hbm.at[last], from_bi, 1, 1, 4)
-
-    def hops(offset, length):
-        return min(offset, length - offset)
 
     def post(dx, dy, dn):
         device = partner(dx, dy, dn)
@@ -371,15 +369,8 @@
             device_id_type=MESH,
         ).start()
 
-    for dx, dy in sorted(
-        [(0, 0)] + far_offsets, key=lambda o: -(hops(o[0], wide) + hops(o[1], blocks))
-    ):
-        def post_near(k, _):
-            post(dx, dy, lax.rem(k + 3, NEAR))
-            return _
-
-        own = int(dx == 0 and dy == 0)
-        lax.fori_loop(0, NEAR - own, post_near if not own else lambda k, _: (post(0, 0, k + 1), _)[1], 0)
+    for offset in offsets:
+        post(*offset)
 
     loads[0].wait()
     take_row(p, 0, first_x)
@@ -628,7 +619,7 @@
             VMEM(traces.shape, F32), VMEM((1, held), jnp.int32), VMEM((1, held), jnp.int32),
             VMEM(resample.shape, F32),
         ]
-        + [dma((6,)), dma((4,)), dma((8,)), dma((8,)), dma, dma, pltpu.SemaphoreType.REGULAR],
+        + [dma((6,)), dma((4,)), dma((8,)), dma((8,)), dma, dma],
         compiler_params=pltpu.CompilerParams(collective_id=0, has_side_effects=True, vmem_limit_bytes=8 * MIB),
         name="route",
     )(

time: 41 us -> 39 us (0.951)
  Pallas kernels: 40.3 us -> 38.6 us
    pallas_call x1, Pallas kernels: 16.8 us -> 15 us  [shards(): pl.pallas_call(route, out_shape=[VMEM(field, F32)] * 6 + [VMEM(plane, F32...]
where the time goes in v6:
time: 39 us; the launch traced here: 39.3 us
  Pallas kernels  38.6 us (99%)
  between operations  0.66 us (2%)
    pallas_call x1, Pallas kernels, shards(): pl.pallas_call(route, out_shape=[VMEM(field, F32)] * 6 + [VMEM(plane, F32...  15 us
    pallas_call x1, Pallas kernels, shards(): pl.pallas_call(advance, out_shape=[VMEM(field, F32)] * 4 + [VMEM(plane, F...  14.3 us
    pallas_call x1, Pallas kernels, shards(): pl.pallas_call(scatter, out_shape=[VMEM(injection, F32)] * 2, in_specs=[v...  5.96 us
    pallas_call x1, Pallas kernels, shards(): pl.pallas_call(finish, out_shape=[HBM(field, F32)] * 4, in_specs=[vmem] *...  3.35 us

profile of v6, /device:TPU:8, one launch (start us, length us, event | category | flops | bytes accessed | tf_op | source)
XLA Modules:
  0.0 39.3 jit_solution(5628501646327066185)
XLA Ops:
  0.6 15.0 %route.1 = (f32[32,64,256]{2,1,0:T(8,128)S(1)}, f32[32,64,256]{2,1,0:T(8,128)S(1)}, f32[32,64,256]{2,1,0:T(8,128)S(1)}, f32[32,64,256]{2,1,0:T(8,128)S(1)}, f32[...) custom-call(f32[32,64,256]{2,1,0:T(8,128)} %p_hbm.1, ...), custom_call_target="tpu_custom_call" | custom-call | tf_op jit(solution)/shard_map/route/pallas_call | solution.py:605
  15.7 6.0 %scatter.1 = (f32[16384,128]{1,0:T(8,128)S(1)}, f32[16384,128]{1,0:T(8,128)S(1)}) custom-call(s32[16,128]{1,0:T(8,128)S(1)} %get-tuple-element.36.index_ref, f32[128,128]{1,0:T(8,128)S(1)} %get-tuple-element.37.values, f32[16384,128]{1,0:T(8,128)S(1)} %get-tuple-element.38._a, ...), custom_call_target="tpu_custom_call", output_to_operand_aliasing={{0}: (2, {}), {1}: (3, {})} | custom-call | tf_op jit(solution)/shard_map/scatter/pallas_call | solution.py:635
  21.6 14.3 %advance.1 = (f32[32,64,256]{2,1,0:T(8,128)S(1)}, f32[32,64,256]{2,1,0:T(8,128)S(1)}, f32[32,64,256]{2,1,0:T(8,128)S(1)}, f32[32,64,256]{2,1,0:T(8,128)S(1)}, f3...) custom-call(f32[32,64,256]{2,1,0:T(8,128)S(1)} %get-tuple-element.26.p_in, f32[32,64,256]{2,1,0:T(8,128)S(1)} %get-tuple-element.27.vi_in, ...), custom_call_target="tpu_custom_call" | custom-call | tf_op jit(solution)/shard_map/advance/pallas_call | solution.py:646
  35.9 3.4 %finish.1 = (f32[32,64,256]{2,1,0:T(8,128)}, f32[32,64,256]{2,1,0:T(8,128)}, f32[32,64,256]{2,1,0:T(8,128)}, f32[32,64,256]{2,1,0:T(8,128)}) custom-call(f32[32,64,256]{2,1,0:T(8,128)S(1)} %get-tuple-element.42.p_in, f32[32,64,256]{2,1,0:T(8,128)S(1)} %get-tuple-element.43.vi, f32[32,64,256]{2,1,0:T(8,128)S(1)} %get-tuple-element.44.vx, ...), custom_call_target="tpu_custom_call" | custom-call | tf_op jit(solution)/shard_map/finish/pallas_call | solution.py:660

commit v7 on v6

--- a/solution.py
+++ b/solution.py
@@ -284,7 +284,6 @@
     devices = lax.axis_size("xline") * lax.axis_size("inline")
     lines = lax.axis_size("inline")
     planes, tiles = p.shape[0], p.shape[1] // SUBLANES
-    injected = (injected_a, injected_b)
     loads = [
         pltpu.make_async_copy(source, target, load_sems.at[k])
         for k, (source, target) in enumerate(
@@ -384,12 +383,14 @@
     take_row(vx, p.shape[1] - 1, last_vx)
     halo.send(last_vx, from_vx, 0, 1, 7)
 
-    def clear(k, _):
-        for ref in injected:
+    def clear(ref):
+        def part(k, _):
             ref[pl.ds(pl.multiple_of(k * 64, 64), 64), :] = jnp.zeros((64, LANES), F32)
-        return _
-
-    lax.fori_loop(0, injected[0].shape[0] // 64, clear, 0)
+            return _
+
+        lax.fori_loop(0, ref.shape[0] // 64, part, 0)
+
+    clear(injected_a)
     loads[3].wait()
     loads[4].wait()
     v = (vi, vx, vd)
@@ -400,6 +401,7 @@
         pressure(p, p, v, (ghost_i, ghost_x), modulus, i, tile, first, None)
 
     core(planes, tiles, strip)
+    clear(injected_b)
     halo.finish()
     velocity_next(p, v, v, buoyancy, ahead_i)
     for i in (0, planes - 1):

time: 39 us -> 39.8 us (1.021)
  Pallas kernels: 38.6 us -> 39.2 us
    pallas_call x1, Pallas kernels: 15 us -> 16 us  [shards(): pl.pallas_call(route, out_shape=[VMEM(field, F32)] * 6 + [VMEM(plane, F32...]
where the time goes in v7:
time: 39.8 us; the launch traced here: 39.9 us
  Pallas kernels  39.2 us (98%)
  between operations  0.66 us (2%)
    pallas_call x1, Pallas kernels, shards(): pl.pallas_call(route, out_shape=[VMEM(field, F32)] * 6 + [VMEM(plane, F32...  16 us
    pallas_call x1, Pallas kernels, shards(): pl.pallas_call(advance, out_shape=[VMEM(field, F32)] * 4 + [VMEM(plane, F...  14.3 us
    pallas_call x1, Pallas kernels, shards(): pl.pallas_call(scatter, out_shape=[VMEM(injection, F32)] * 2, in_specs=[v...  5.65 us
    pallas_call x1, Pallas kernels, shards(): pl.pallas_call(finish, out_shape=[HBM(field, F32)] * 4, in_specs=[vmem] *...  3.35 us

profile of v7, /device:TPU:8, one launch (start us, length us, event | category | flops | bytes accessed | tf_op | source)
XLA Modules:
  0.0 39.9 jit_solution(11652327576377268581)
XLA Ops:
  0.6 16.0 %route.1 = (f32[32,64,256]{2,1,0:T(8,128)S(1)}, f32[32,64,256]{2,1,0:T(8,128)S(1)}, f32[32,64,256]{2,1,0:T(8,128)S(1)}, f32[32,64,256]{2,1,0:T(8,128)S(1)}, f32[...) custom-call(f32[32,64,256]{2,1,0:T(8,128)} %p_hbm.1, ...), custom_call_target="tpu_custom_call" | custom-call | tf_op jit(solution)/shard_map/route/pallas_call | solution.py:607
  16.6 5.6 %scatter.1 = (f32[16384,128]{1,0:T(8,128)S(1)}, f32[16384,128]{1,0:T(8,128)S(1)}) custom-call(s32[16,128]{1,0:T(8,128)S(1)} %get-tuple-element.36.index_ref, f32[128,128]{1,0:T(8,128)S(1)} %get-tuple-element.37.values, f32[16384,128]{1,0:T(8,128)S(1)} %get-tuple-element.38._a, ...), custom_call_target="tpu_custom_call", output_to_operand_aliasing={{0}: (2, {}), {1}: (3, {})} | custom-call | tf_op jit(solution)/shard_map/scatter/pallas_call | solution.py:637
  22.3 14.3 %advance.1 = (f32[32,64,256]{2,1,0:T(8,128)S(1)}, f32[32,64,256]{2,1,0:T(8,128)S(1)}, f32[32,64,256]{2,1,0:T(8,128)S(1)}, f32[32,64,256]{2,1,0:T(8,128)S(1)}, f3...) custom-call(f32[32,64,256]{2,1,0:T(8,128)S(1)} %get-tuple-element.26.p_in, f32[32,64,256]{2,1,0:T(8,128)S(1)} %get-tuple-element.27.vi_in, ...), custom_call_target="tpu_custom_call" | custom-call | tf_op jit(solution)/shard_map/advance/pallas_call | solution.py:648
  36.6 3.4 %finish.1 = (f32[32,64,256]{2,1,0:T(8,128)}, f32[32,64,256]{2,1,0:T(8,128)}, f32[32,64,256]{2,1,0:T(8,128)}, f32[32,64,256]{2,1,0:T(8,128)}) custom-call(f32[32,64,256]{2,1,0:T(8,128)S(1)} %get-tuple-element.42.p_in, f32[32,64,256]{2,1,0:T(8,128)S(1)} %get-tuple-element.43.vi, f32[32,64,256]{2,1,0:T(8,128)S(1)} %get-tuple-element.44.vx, ...), custom_call_target="tpu_custom_call" | custom-call | tf_op jit(solution)/shard_map/finish/pallas_call | solution.py:662
